TPU v7x, 256 devices: a whole 4x4x8 slice. The times are simulated.
256 devices in a mesh: mass: 64 (over z, x, core), sub: 4 (over y).
Axes of the slice: x: 4, y: 4, z: 8, core: 2. Of those that a mesh axis runs over, the one named last changes fastest.
Arguments:
- queries: bfloat16 [1024, 32, 1024], P('mass'), may hold values from -6 to 6
- query_mass: int32 [1024, 32], P('mass'), may hold values from 0 to 47
- first_range: int32 [1024], P('mass'), may hold values from 0 to 61, as said below
- library: bfloat16 [32768, 1024], P(('mass', 'sub')), may hold values from -6 to 6
- library_mass: int32 [32768], P(('mass', 'sub')), may hold values from 0 to 15, as said below
- shuffle: int32 [1024], replicated, may hold values from 0 to 1023, each once
Outputs:
- target_best: float32 [1024, 5, 32], P('mass')
- decoy_best: float32 [1024, 5, 32], P('mass')
Inputs may be any that keep to these rules, and one draw needn't show every extreme that they name: Within each aligned run of 16 blocks the mass ranges first_range to first_range + 2 of different blocks are disjoint. `library_mass`: every mass range holds exactly 32 spectra at each bin.
All inputs are finite; a program needn't handle non-finite values.
Results may differ from a plain program's by a relative error of at most 0.0003.
Values may be sent and summed in bfloat16 or wider, within the bound.
A program may use at most 64 MiB of HBM per device.

v0:
```python
import jax
import jax.numpy as jnp
from jax import lax
from jax.sharding import PartitionSpec as P

BINS = 16
TOLERANCE = 4
WINDOW = 3
TOP_HITS = 5


epsilon = 1e-06
floor_score = -3.0


def from_everyone(array, axis):
    copies = jnp.broadcast_to(array, (lax.axis_size(axis), *array.shape))
    return lax.all_to_all(copies, axis, split_axis=0, concat_axis=0, tiled=True)


def folded_in_pairs(pieces, combine):
    while len(jax.tree.leaves(pieces)[0]) > 1:
        pieces = jax.vmap(combine)(
            *(jax.tree.map(lambda part: part[side::2], pieces) for side in (0, 1))
        )
    return jax.tree.map(lambda part: part[0], pieces)


def combined_all(array, axis, combine):
    pieces = jax.tree.map(lambda part: from_everyone(part, axis), array)
    return folded_in_pairs(pieces, combine)


def best_of(values):
    ordered = -jnp.sort(-values, axis=1)
    return ordered[:, :TOP_HITS]


def join_lanes(former, latter):
    target_lane = best_of(jnp.concatenate([former[0], latter[0]], axis=1))
    decoy_lane = best_of(jnp.concatenate([former[1], latter[1]], axis=1))
    return (target_lane, decoy_lane)


def score_lanes(query_rows, rows_mass, spectra, spectra_mass, shuffle):
    spectra_scale = lax.rsqrt(
        jnp.einsum("ld,ld->l", spectra, spectra, preferred_element_type=jnp.float32) + epsilon
    )
    rows_scale = lax.rsqrt(
        jnp.einsum("srd,srd->sr", query_rows, query_rows, preferred_element_type=jnp.float32)
        + epsilon
    )
    allowed = jnp.abs(rows_mass[:, :, None] - spectra_mass[None, None, :]) <= TOLERANCE
    shuffled = jnp.take(spectra, shuffle, axis=1)
    factor = rows_scale[:, :, None] * spectra_scale[None, None, :]
    target_score = (
        jnp.einsum("srd,ld->srl", query_rows, spectra, preferred_element_type=jnp.float32) * factor
    )
    decoy_score = (
        jnp.einsum("srd,ld->srl", query_rows, shuffled, preferred_element_type=jnp.float32) * factor
    )
    target_score = jnp.where(allowed, target_score, floor_score)
    decoy_score = jnp.where(allowed, decoy_score, floor_score)
    target_lane = jnp.transpose(lax.top_k(target_score, TOP_HITS)[0], (0, 2, 1))
    decoy_lane = jnp.transpose(lax.top_k(decoy_score, TOP_HITS)[0], (0, 2, 1))
    return (target_lane, decoy_lane)


def per_device(queries, query_mass, first_range, library, library_mass, shuffle):
    mass_count = lax.axis_size("mass")
    own_range = lax.axis_index("mass")
    block_count = queries.shape[0]
    targets = jnp.arange(mass_count, dtype=jnp.int32)
    covers = (first_range[None, :] <= targets[:, None]) & (
        targets[:, None] < first_range[None, :] + WINDOW
    )
    filled = jnp.any(covers, axis=1)
    block_ids = jnp.arange(block_count, dtype=jnp.int32)
    chosen = jnp.sum(jnp.where(covers, block_ids[None, :], 0), axis=1)
    outgoing = jnp.take(queries, chosen, axis=0)
    outgoing_mass = (
        jnp.take(query_mass, chosen, axis=0) + (jnp.take(first_range, chosen) * BINS)[:, None]
    )
    outgoing_mass = jnp.where(filled[:, None], outgoing_mass, -1000 * BINS)
    spectra_mass = own_range * BINS + library_mass
    incoming, incoming_mass = (
        lax.all_to_all(outgoing, "mass", split_axis=0, concat_axis=0, tiled=True),
        lax.all_to_all(outgoing_mass, "mass", split_axis=0, concat_axis=0, tiled=True),
    )
    best_lanes = score_lanes(incoming, incoming_mass, library, spectra_mass, shuffle)
    best_lanes = combined_all(best_lanes, "sub", join_lanes)
    back_target, back_decoy = (
        lax.all_to_all(best_lanes[0], "mass", split_axis=0, concat_axis=0, tiled=True),
        lax.all_to_all(best_lanes[1], "mass", split_axis=0, concat_axis=0, tiled=True),
    )
    windows = (first_range[:, None] + jnp.arange(WINDOW, dtype=jnp.int32)[None, :]).reshape(-1)

    def settle(lane_block):
        picked = jnp.take(lane_block, windows, axis=0)
        picked = picked.reshape(block_count, WINDOW * TOP_HITS, lane_block.shape[2])
        return best_of(picked)

    target_best = settle(back_target)
    decoy_best = settle(back_decoy)
    return (target_best, decoy_best)


def solution(mesh):
    return jax.shard_map(
        per_device,
        mesh=mesh,
        in_specs=(
            P("mass", None, None),
            P("mass", None),
            P("mass"),
            P(("mass", "sub"), None),
            P(("mass", "sub")),
            P(),
        ),
        out_specs=(P("mass", None, None), P("mass", None, None)),
        check_vma=False,
    )
```

profile of v0, /device:TPU:1, one launch (start us, length us, event | category | flops | bytes accessed | tf_op | source)
XLA Modules:
  0.0 559.6 jit_solution(13619992955288376718)
XLA Ops:
  0.6 0.7 broadcast_add_fusion.1
  1.4 0.7 select_reduce_fusion
  2.2 1.4 gather_fusion.1
  3.6 2.8 gather_fusion.2
  6.4 4.6 broadcast_select_fusion
  11.0 13.3 %all-to-all-start.1 = ((bf16[64,32,1024]{2,1,0:T(8,128)(2,1)}), bf16[64,32,1024]{2,1,0:T(8,128)(2,1)}, u32[]{:S(2)}, u32[]{:S(2)}) async-start(bf16[64,32,1024]{2,1,0:T(8,128)(2,1)} %broadcast_select_fusion), calls=%async_computation.1 | async-start | bytes 8388608 | tf_op jit(solution)/shard_map/all_to_all | solution.py:87
  24.3 0.6 gather_fusion
  24.9 0.2 copy.79
  25.1 0.1 iota_add_fusion
  25.2 0.1 add.116
  25.3 3.2 gather_fusion.3
  28.5 0.1 fusion.14
  28.6 0.1 fusion.3
  28.8 0.7 fusion.12
  29.5 89.5 %all-to-all-done.1 = bf16[64,32,1024]{2,1,0:T(8,128)(2,1)} async-done(((bf16[64,32,1024]{2,1,0:T(8,128)(2,1)}), bf16[64,32,1024]{2,1,0:T(8,128)(2,1)}, u32[]{:S(2)}, u32[]{:S(2)}) %all-to-all-start.1) | async-done | bytes 4194336 | tf_op jit(solution)/shard_map/all_to_all | solution.py:87
  119.0 6.8 %all-to-all-start = ((s32[64,1,32]{2,1,0:T(1,128)}), s32[64,1,32]{2,1,0:T(1,128)S(1)}, u32[]{:S(2)}, u32[]{:S(2)}) async-start(s32[64,1,32]{2,1,0:T(1,128)} %bitcast.3), calls=%async_computation | async-start | bytes 65536 | tf_op jit(solution)/shard_map/all_to_all | solution.py:88
  125.9 3.1 fusion
  128.9 6.3 %all-to-all-done = s32[64,1,32]{2,1,0:T(1,128)S(1)} async-done(((s32[64,1,32]{2,1,0:T(1,128)}), s32[64,1,32]{2,1,0:T(1,128)S(1)}, u32[]{:S(2)}, u32[]{:S(2)}) %all-to-all-start) | async-done | bytes 8224 | tf_op jit(solution)/shard_map/all_to_all | solution.py:88
  135.2 3.6 fusion.1
  138.8 0.1 iota.40
  138.9 141.0 %top_k.20 = (f32[64,32,128]{2,1,0:T(8,128)}, s32[64,32,128]{2,1,0:T(8,128)}) sort(f32[64,32,128]{2,1,0:T(8,128)S(1)} %fusion.1, s32[64,32,128]{2,1,0:T(8,128)S(1)} %iota.40), dimensions={2}, to_apply=%region_6.8 | sort | flops 4718592 | bytes 4194304 | tf_op jit(solution)/shard_map/top_k | solution.py:65
  279.9 1.3 slice_bitcast_fusion
  281.2 0.6 copy.80
  281.8 0.9 reshape.245
  282.7 4.2 all-to-all-start.4
  286.9 3.6 fusion.2
  290.5 0.1 iota.36
  290.6 141.0 %top_k.14 = (f32[64,32,128]{2,1,0:T(8,128)}, s32[64,32,128]{2,1,0:T(8,128)}) sort(f32[64,32,128]{2,1,0:T(8,128)S(1)} %fusion.2, s32[64,32,128]{2,1,0:T(8,128)S(1)} %iota.36), dimensions={2}, to_apply=%region_2.3 | sort | flops 4718592 | bytes 4194304 | tf_op jit(solution)/shard_map/top_k | solution.py:64
  431.6 1.3 slice_bitcast_fusion.1
  432.9 0.6 copy.75
  433.6 0.9 reshape.241
  434.5 4.2 all-to-all-start.2
  438.7 0.5 broadcast.170
  439.2 2.0 reduce.4
  441.2 0.2 reshape.246
  441.5 0.2 copy.81
  441.7 23.9 %sort.88 = (f32[2,64,10,32]{1,2,3,0:T(8,128)S(1)}, s32[2,64,10,32]{1,2,3,0:T(8,128)}) sort(f32[2,64,10,32]{1,2,3,0:T(8,128)S(1)} %copy.81, s32[2,64,10,32]{1,2,3,0:T(8,128)S(1)} %iota.41), dimensions={2}, to_apply=%region_7.9 | sort | flops 655360 | bytes 655360 | tf_op jit(solution)/shard_map/vmap(jit(sort))/sort | solution.py:35
  465.7 0.1 maximum_negate_fusion.3
  465.8 12.1 %sort.89 = (f32[1,64,10,32]{1,2,3,0:T(8,128)S(1)}, s32[1,64,10,32]{1,2,3,0:T(8,128)}) sort(f32[1,64,10,32]{1,2,3,0:T(8,128)S(1)} %maximum_negate_fusion.3, s32[1,64,10,32]{1,2,3,0:T(8,128)S(1)} %iota.42), dimensions={2}, to_apply=%region_8.10 | sort | flops 307200 | bytes 327680 | tf_op jit(solution)/shard_map/vmap(jit(sort))/sort | solution.py:35
  477.8 0.1 copy.82
  477.9 0.1 copy.83
  478.1 0.8 reshape.247
  478.8 5.7 %all-to-all-start.5 = ((f32[64,1,160]{2,1,0:T(1,128)}), f32[64,1,160]{2,1,0:T(1,128)S(1)}, u32[]{:S(2)}, u32[]{:S(2)}) async-start(f32[64,1,160]{2,1,0:T(1,128)} %reshape.247), calls=%async_computation.5 | async-start | bytes 131072 | tf_op jit(solution)/shard_map/all_to_all | solution.py:94
  484.5 1.1 reduce.6
  485.6 0.2 reshape.242
  485.9 0.2 copy.76
  486.2 23.9 %sort.85 = (f32[2,64,10,32]{1,2,3,0:T(8,128)S(1)}, s32[2,64,10,32]{1,2,3,0:T(8,128)}) sort(f32[2,64,10,32]{1,2,3,0:T(8,128)S(1)} %copy.76, s32[2,64,10,32]{1,2,3,0:T(8,128)S(1)} %iota.37), dimensions={2}, to_apply=%region_3.4 | sort | flops 655360 | bytes 655360 | tf_op jit(solution)/shard_map/vmap(jit(sort))/sort | solution.py:35
  510.2 12.1 %sort.86 = (f32[1,64,10,32]{1,2,3,0:T(8,128)S(1)}, s32[1,64,10,32]{1,2,3,0:T(8,128)}) sort(f32[1,64,10,32]{1,2,3,0:T(8,128)S(1)} %maximum_negate_fusion.2, s32[1,64,10,32]{1,2,3,0:T(8,128)S(1)} %iota.38), dimensions={2}, to_apply=%region_4.5 | sort | flops 307200 | bytes 327680 | tf_op jit(solution)/shard_map/vmap(jit(sort))/sort | solution.py:35
  522.3 0.1 copy.77
  522.3 0.1 copy.78
  522.5 0.8 reshape.243
  523.3 10.4 %all-to-all-start.3 = ((f32[64,1,160]{2,1,0:T(1,128)}), f32[64,1,160]{2,1,0:T(1,128)S(1)}, u32[]{:S(2)}, u32[]{:S(2)}) async-start(f32[64,1,160]{2,1,0:T(1,128)} %reshape.243), calls=%async_computation.3 | async-start | bytes 131072 | tf_op jit(solution)/shard_map/all_to_all | solution.py:93
  533.7 0.8 reduce.5
  534.5 0.1 reshape.248
  534.6 9.2 %all-to-all-done.3 = f32[64,1,160]{2,1,0:T(1,128)S(1)} async-done(((f32[64,1,160]{2,1,0:T(1,128)}), f32[64,1,160]{2,1,0:T(1,128)S(1)}, u32[]{:S(2)}, u32[]{:S(2)}) %all-to-all-start.3) | async-done | bytes 40992 | tf_op jit(solution)/shard_map/all_to_all | solution.py:93
  543.8 0.8 reduce.7
  544.6 0.1 reshape.244
  544.7 0.6 gather_fusion.5
  545.3 0.6 gather_fusion.4
  545.9 0.1 select_negate_fusion
  546.1 6.1 %sort.87 = (f32[16,15,32]{2,1,0:T(8,128)S(1)}, s32[16,15,32]{2,1,0:T(8,128)}) sort(f32[16,15,32]{2,1,0:T(8,128)S(1)} %neg.63, s32[16,15,32]{2,1,0:T(8,128)S(1)} %iota.39), dimensions={1}, to_apply=%region_5.7 | sort | flops 99840 | bytes 122880 | tf_op jit(solution)/shard_map/jit(sort)/sort | solution.py:35
  552.2 0.6 copy.84
  552.9 6.1 %sort.90 = (f32[16,15,32]{2,1,0:T(8,128)S(1)}, s32[16,15,32]{2,1,0:T(8,128)}) sort(f32[16,15,32]{2,1,0:T(8,128)S(1)} %neg.70, s32[16,15,32]{2,1,0:T(8,128)S(1)} %iota.43), dimensions={1}, to_apply=%region_9.11 | sort | flops 99840 | bytes 122880 | tf_op jit(solution)/shard_map/jit(sort)/sort | solution.py:35
  559.0 0.6 copy.85
  (49 shorter events, 0.6 us)
Async XLA Ops:
  0.6 3.0 copy-start
  11.0 13.3 %copy-start.2 = (s32[16,32]{1,0:T(8,128)S(1)}, s32[16,32]{1,0:T(8,128)}, u32[]{:S(2)}) copy-start(s32[16,32]{1,0:T(8,128)} %param.9) | copy-start | bytes 6148
  11.0 13.9 %copy-start.3 = (bf16[128,1024]{1,0:T(8,128)(2,1)S(1)}, bf16[128,1024]{1,0:T(8,128)(2,1)}, u32[]{:S(2)}) copy-start(bf16[128,1024]{1,0:T(8,128)(2,1)} %param.11) | copy-start | bytes 786436
  11.0 14.1 %copy-start.1 = (s32[16]{0:T(128)S(1)}, s32[16]{0:T(128)}, u32[]{:S(2)}) copy-start(s32[16]{0:T(128)} %param.10) | copy-start | bytes 196
  11.0 14.3 %copy-start.4 = (s32[1024]{0:T(1024)S(1)}, s32[1024]{0:T(1024)}, u32[]{:S(2)}) copy-start(s32[1024]{0:T(1024)} %param.13) | copy-start | bytes 12292
  11.0 17.8 %copy-start.5 = (s32[128]{0:T(128)S(1)}, s32[128]{0:T(128)}, u32[]{:S(2)}) copy-start(s32[128]{0:T(128)} %param.12) | copy-start | bytes 1540
  11.0 108.0 %all-to-all-start.1 = ((bf16[64,32,1024]{2,1,0:T(8,128)(2,1)}), bf16[64,32,1024]{2,1,0:T(8,128)(2,1)}, u32[]{:S(2)}, u32[]{:S(2)}) async-start(bf16[64,32,1024]{2,1,0:T(8,128)(2,1)} %broadcast_select_fusion), calls=%async_computation.1 | async-start | bytes 8388608 | tf_op jit(solution)/shard_map/all_to_all | solution.py:87
  119.0 16.2 %all-to-all-start = ((s32[64,1,32]{2,1,0:T(1,128)}), s32[64,1,32]{2,1,0:T(1,128)S(1)}, u32[]{:S(2)}, u32[]{:S(2)}) async-start(s32[64,1,32]{2,1,0:T(1,128)} %bitcast.3), calls=%async_computation | async-start | bytes 65536 | tf_op jit(solution)/shard_map/all_to_all | solution.py:88
  282.7 151.8 %all-to-all-start.4 = ((f32[4,1,10240]{2,1,0:T(1,128)}), f32[4,1,10240]{2,1,0:T(1,128)}, u32[]{:S(2)}, u32[]{:S(2)}) async-start(f32[4,1,10240]{2,1,0:T(1,128)} %reshape.245), calls=%async_computation.4 | async-start | bytes 327680 | tf_op jit(solution)/shard_map/all_to_all | solution.py:18
  434.5 44.4 %all-to-all-start.2 = ((f32[4,1,10240]{2,1,0:T(1,128)}), f32[4,1,10240]{2,1,0:T(1,128)S(1)}, u32[]{:S(2)}, u32[]{:S(2)}) async-start(f32[4,1,10240]{2,1,0:T(1,128)} %reshape.241), calls=%async_computation.2 | async-start | bytes 327680 | tf_op jit(solution)/shard_map/all_to_all | solution.py:18
  478.8 44.4 %all-to-all-start.5 = ((f32[64,1,160]{2,1,0:T(1,128)}), f32[64,1,160]{2,1,0:T(1,128)S(1)}, u32[]{:S(2)}, u32[]{:S(2)}) async-start(f32[64,1,160]{2,1,0:T(1,128)} %reshape.247), calls=%async_computation.5 | async-start | bytes 131072 | tf_op jit(solution)/shard_map/all_to_all | solution.py:94
  523.3 20.5 %all-to-all-start.3 = ((f32[64,1,160]{2,1,0:T(1,128)}), f32[64,1,160]{2,1,0:T(1,128)S(1)}, u32[]{:S(2)}, u32[]{:S(2)}) async-start(f32[64,1,160]{2,1,0:T(1,128)} %reshape.243), calls=%async_computation.3 | async-start | bytes 131072 | tf_op jit(solution)/shard_map/all_to_all | solution.py:93
where the time goes:
time: 560 us
  other arithmetic  381 us (68%)
  waiting for transfers between devices  105 us (19%)
  starting transfers between devices  44.6 us (8%)
  local copies, waits for them, and re-layouts  20.4 us (4%)
  matrix products  7.15 us (1%)
    top_k x1, other arithmetic, score_lanes(): target_lane = jnp.transpose(lax.top_k(target_score, TOP_HITS)[0], (0, 2, 1))  141 us
    top_k x1, other arithmetic, score_lanes(): decoy_lane = jnp.transpose(lax.top_k(decoy_score, TOP_HITS)[0], (0, 2, 1))  141 us
    all_to_all x1, waiting for transfers between devices, per_device(): lax.all_to_all(outgoing, 'mass', split_axis=0, concat_axis=0, tiled=True)  89.5 us
    sort x6, other arithmetic, best_of(): ordered = -jnp.sort(-values, axis=1)  84.1 us
    all_to_all x1, starting transfers between devices, per_device(): lax.all_to_all(outgoing, 'mass', split_axis=0, concat_axis=0, tiled=True)  13.3 us
  transfers between devices with their start and end apart: 6, of which 3 were waited for; matrix products, arithmetic and copies ran while one was open for 42% of the time, Pallas kernels for 0%

commit v1 on v0

v1 whole, which is shorter than its diff:
```python
import functools

import jax
import jax.numpy as jnp
from jax import lax
from jax.experimental import pallas as pl
from jax.experimental.pallas import tpu as pltpu
from jax.sharding import PartitionSpec as P

BINS = 16
TOLERANCE = 4
WINDOW = 3
TOP_HITS = 5
NZ, NX, NC, NY = 8, 4, 2, 4
CHIPS = NZ * NX
SLOTS = 4
ROWS = 8
LANES = 128
OFFSET = 64.0
epsilon = 1e-06
floor_score = -3.0
EMPTY = -1e30
MESH = pl.DeviceIdType.MESH
Z_ORDER = (4, 3, 5, 2, 6, 1, 7)


def insert(best, new, start=0):
    best = list(best)
    for k in range(start, TOP_HITS):
        high = jnp.maximum(best[k], new)
        if k + 1 < TOP_HITS:
            new = jnp.minimum(best[k], new)
        best[k] = high
    return best


def merged(former, latter):
    for k in range(TOP_HITS):
        former = insert(former, latter[k], k)
    return former


def swap_blocks(table):
    row = lax.broadcasted_iota(jnp.int32, table.shape, 0)
    segment = lax.broadcasted_iota(jnp.int32, table.shape, 1) // ROWS
    for bit in range(4):
        step = 1 << bit
        up = pltpu.roll(pltpu.roll(table, 16 - step, 0), ROWS * step, 1)
        down = pltpu.roll(pltpu.roll(table, step, 0), LANES - ROWS * step, 1)
        row_bit = (row // step) % 2
        segment_bit = (segment // step) % 2
        table = jnp.where(row_bit == segment_bit, table, jnp.where(row_bit == 0, up, down))
    return table


def search_kernel(
    first_ref, send, msg, lib, lib_mass, shuffle, q_scale, out,
    zbuf, qbuf, mbuf, lbuf, lmbuf, decoy, onehot, qsel, scale_rep, mass_rep,
    score_t, score_d, obuf, rbuf, abuf, fin, ybuf,
    z_send, z_recv, x_send, x_recv, m_send, m_recv, r_send, r_recv,
    l_send, l_recv, c_send, c_recv, lm_send, lm_recv, y_send, y_recv, here_sem,
):
    m = lax.axis_index("mass")
    y = lax.axis_index("sub")
    depth = lib.shape[1]
    lib_rows = lib.shape[0]
    range_rows = NY * lib_rows
    z = m // (NX * NC)
    x = (m // NC) % NX
    c = m % NC
    g = m // NC
    partner = m + 1 - 2 * c

    def device(chip):
        return (chip * NC + c, y)

    def turn(value, step, count):
        return lax.rem(value + step, count)

    barrier = pltpu.get_barrier_semaphore()

    def greet(k, carry):
        pl.semaphore_signal(barrier, inc=1, device_id=device(turn(g, k, CHIPS)), device_id_type=MESH)
        return carry

    lax.fori_loop(1, CHIPS, greet, 0)
    for step in range(1, NY):
        pl.semaphore_signal(barrier, inc=1, device_id=(m, turn(y, step, NY)), device_id_type=MESH)
    for step in range(NY):
        pl.semaphore_signal(barrier, inc=1, device_id=(partner, turn(y, step, NY)), device_id_type=MESH)
    pl.semaphore_wait(barrier, CHIPS - 1 + NY - 1 + NY)

    def remote(src, dst, send_sem, recv_sem, target):
        return pltpu.make_async_remote_copy(
            src_ref=src, dst_ref=dst, send_sem=send_sem, recv_sem=recv_sem,
            device_id=target, device_id_type=MESH,
        )

    def z_copy(dz):
        zt = turn(z, dz, NZ)
        return remote(
            send.at[pl.ds(zt * SLOTS, SLOTS)], zbuf.at[z], z_send.at[dz], z_recv.at[dz],
            device(zt * NX + x),
        )

    def pair_of(xt):
        return jnp.maximum(xt - 1, 0)

    def x_copy(dz, dx):
        zs = turn(z, NZ - dz, NZ)
        xt = turn(x, dx, NX)
        if dz == 0:
            src = send.at[pl.ds(z * SLOTS + pair_of(xt), 2)]
        else:
            src = zbuf.at[zs, pl.ds(pair_of(xt), 2)]
        if dx == 0:
            return pltpu.make_async_copy(src, qbuf.at[zs, x], here_sem.at[dz])
        return remote(
            src, qbuf.at[zs, x], x_send.at[dz, dx], x_recv.at[dz, dx], device(z * NX + xt)
        )

    for dz in Z_ORDER:
        z_copy(dz).start()
    for dx in (2, 1, 3, 0):
        x_copy(0, dx).start()

    half = lib_rows // 2
    up, down, opposite = turn(y, 1, NY), turn(y, NY - 1, NY), turn(y, 2, NY)
    own_keep = pltpu.make_async_copy(lib, lbuf.at[c, y], here_sem.at[NZ])
    own_up = remote(lib, lbuf.at[c, y], l_send.at[0], l_recv.at[0], (m, up))
    own_down = remote(lib, lbuf.at[c, y], l_send.at[1], l_recv.at[1], (m, down))
    own_core = remote(lib, lbuf.at[c, y], c_send.at[0], c_recv.at[0], (partner, y))
    own_up.start()
    own_down.start()
    own_core.start()
    own_keep.start()

    def mass_copy(k, carry):
        chip = turn(g, k, CHIPS)
        remote(msg.at[chip], mbuf.at[g], m_send, m_recv, device(chip)).start()
        return carry

    lax.fori_loop(1, CHIPS, mass_copy, 0)
    mass_keep = pltpu.make_async_copy(msg.at[g], mbuf.at[g], here_sem.at[NZ + 1])
    mass_keep.start()
    lm_keep = pltpu.make_async_copy(lib_mass, lmbuf.at[c, y], here_sem.at[NZ + 2])
    lm_keep.start()
    lm_copies = []
    for core in range(NC):
        for step in range(NY):
            if core == 0 and step == 0:
                continue
            at = core * NY + step
            lm_copies.append(remote(
                lib_mass, lmbuf.at[c, y], lm_send.at[at], lm_recv.at[at],
                (m if core == 0 else partner, turn(y, step, NY)),
            ))
    for copy in lm_copies:
        copy.start()

    chunk = 64
    names = shuffle[...]

    def build(i, carry):
        base = pl.multiple_of(i * chunk, chunk)
        index = lax.broadcasted_iota(jnp.int32, (chunk, depth), 0) + base
        onehot[pl.ds(base, chunk), :] = jnp.where(index == names, 1.0, 0.0).astype(jnp.bfloat16)
        return carry

    lax.fori_loop(0, depth // chunk, build, 0)

    for dz in Z_ORDER:
        z_copy(dz).wait_recv()
        for dx in (2, 1, 3, 0):
            x_copy(dz, dx).start()

    own_up.wait_recv()
    relay_up = remote(
        lbuf.at[c, down, pl.ds(0, half)], lbuf.at[c, down, pl.ds(0, half)],
        l_send.at[2], l_recv.at[2], (m, up),
    )
    relay_up.start()
    core_down = remote(lbuf.at[c, down], lbuf.at[c, down], c_send.at[1], c_recv.at[1], (partner, y))
    core_down.start()
    own_down.wait_recv()
    relay_down = remote(
        lbuf.at[c, up, pl.ds(half, half)], lbuf.at[c, up, pl.ds(half, half)],
        l_send.at[3], l_recv.at[3], (m, down),
    )
    relay_down.start()
    core_up = remote(lbuf.at[c, up], lbuf.at[c, up], c_send.at[2], c_recv.at[2], (partner, y))
    core_up.start()
    relay_up.wait_recv()
    relay_down.wait_recv()
    core_opposite = remote(
        lbuf.at[c, opposite], lbuf.at[c, opposite], c_send.at[3], c_recv.at[3], (partner, y)
    )
    core_opposite.start()

    own_keep.wait()
    lm_keep.wait()
    mass_keep.wait()
    for copy in lm_copies:
        copy.wait()
    for copy in (own_core, core_down, core_up, core_opposite):
        copy.wait()
    for copy in (own_up, own_down, relay_up, relay_down):
        copy.wait_send()
    for sem in (m_send, m_recv):
        pltpu.make_async_copy(msg.at[pl.ds(0, CHIPS - 1)], mbuf.at[pl.ds(0, CHIPS - 1)], sem).wait()

    def prepare(i, carry):
        e = i // NY
        piece = i % NY
        base = pl.multiple_of(piece * lib_rows, lib_rows)
        spectra = lbuf[e, piece]
        wide = spectra.astype(jnp.float32)
        total = jnp.sum(wide * wide, axis=1, keepdims=True)
        scale_rep[e, pl.ds(base, lib_rows), :] = jnp.broadcast_to(
            lax.rsqrt(total + epsilon), (lib_rows, LANES)
        )
        mass = jnp.broadcast_to(lmbuf[e, piece], (lib_rows, LANES)).T
        mass_rep[e, pl.ds(base, lib_rows), :] = mass + ((g * NC + e) * BINS).astype(jnp.float32)
        decoy[e, pl.ds(base, lib_rows), :] = jnp.dot(
            spectra, onehot[...], preferred_element_type=jnp.float32
        ).astype(jnp.bfloat16)
        return carry

    lax.fori_loop(0, NC * NY, prepare, 0)

    for dz in (0,) + Z_ORDER:
        for dx in range(NX):
            if dx:
                x_copy(dz, dx).wait()
            else:
                x_copy(dz, dx).wait()
        if dz:
            z_copy(dz).wait_send()

    row8 = lax.broadcasted_iota(jnp.int32, (ROWS, LANES), 0)
    for e in range(NC):
        def choose(i, carry):
            zs = i // 2
            xs = (i % 2) * 2
            codes = mbuf[pl.ds(i * 2, 2), e]
            code = jnp.max(codes, axis=-1, keepdims=True)
            odd = code - 2.0 * jnp.floor(code * 0.5)
            first = qbuf[zs, pl.ds(xs, 2), 0].astype(jnp.float32)
            second = qbuf[zs, pl.ds(xs, 2), 1].astype(jnp.float32)
            picked = jnp.where(odd > 0.5, second, first)
            base = pl.multiple_of(i * 16, 16)
            qsel[pl.ds(base, 16), :] = picked.reshape(2 * ROWS, depth).astype(jnp.bfloat16)
            return carry

        lax.fori_loop(0, CHIPS // 2, choose, 0)

        def score(i, carry):
            base = pl.multiple_of(i * lib_rows, lib_rows)
            block = qsel[...]
            score_t[pl.ds(base, lib_rows), :] = lax.dot_general(
                lbuf[e, i], block, (((1,), (1,)), ((), ())), preferred_element_type=jnp.float32
            )
            score_d[pl.ds(base, lib_rows), :] = lax.dot_general(
                decoy[e, pl.ds(base, lib_rows), :], block, (((1,), (1,)), ((), ())),
                preferred_element_type=jnp.float32,
            )
            return carry

        lax.fori_loop(0, NY, score, 0)

        for lg in range(2):
            codes = mbuf[pl.ds(lg * 16, 16), e]
            code = jnp.sum(codes, axis=0)
            q_mass = jnp.broadcast_to(jnp.floor(code * 0.5) - OFFSET, (ROWS, LANES))

            def scan(i, best):
                base = pl.multiple_of(i * ROWS, ROWS)
                scale = scale_rep[e, pl.ds(base, ROWS), :]
                mass = mass_rep[e, pl.ds(base, ROWS), :]
                allowed = jnp.abs(q_mass - mass) <= TOLERANCE
                target = score_t[pl.ds(base, ROWS), lg * LANES:(lg + 1) * LANES] * scale
                shuffled = score_d[pl.ds(base, ROWS), lg * LANES:(lg + 1) * LANES] * scale
                target = insert(best[:TOP_HITS], jnp.where(allowed, target, EMPTY))
                shuffled = insert(best[TOP_HITS:], jnp.where(allowed, shuffled, EMPTY))
                return tuple(target + shuffled)

            nothing = jnp.full((ROWS, LANES), EMPTY, jnp.float32)
            best = lax.fori_loop(
                0, range_rows // ROWS, scan, (nothing,) * (2 * TOP_HITS), unroll=4
            )
            lanes = []
            for part in (list(best[:TOP_HITS]), list(best[TOP_HITS:])):
                for shift in (4, 2, 1):
                    part = merged(part, [pltpu.roll(v, shift, 0) for v in part])
                lanes += part
            upper = lanes[0]
            for k in range(1, 8):
                upper = jnp.where(row8 == k, lanes[k], upper)
            lower = jnp.where(row8 == 0, lanes[8], lanes[9])
            table = swap_blocks(jnp.concatenate([upper, lower], axis=0))
            for k in range(16):
                obuf[lg * 16 + k, e] = table[k:k + 1, :]

    def result_copy(k, carry):
        chip = turn(g, k, CHIPS)
        remote(obuf.at[chip], rbuf.at[pl.ds(g * 2, 2)], r_send, r_recv, device(chip)).start()
        return carry

    lax.fori_loop(1, CHIPS, result_copy, 0)
    result_keep = pltpu.make_async_copy(obuf.at[g], rbuf.at[pl.ds(g * 2, 2)], here_sem.at[NZ + 3])
    result_keep.start()
    result_keep.wait()
    for sem in (r_send, r_recv):
        pltpu.make_async_copy(
            rbuf.at[pl.ds(0, 2 * (CHIPS - 1))], rbuf.at[pl.ds(0, 2 * (CHIPS - 1))], sem
        ).wait()

    blocks = q_scale.shape[0]
    for b in range(blocks):
        start = first_ref[b]
        for w in range(WINDOW):
            abuf[w, b:b + 1, :] = rbuf[start + w]
    best = None
    for w in range(WINDOW):
        rows = abuf[w]
        parts = [rows] + [pltpu.roll(rows, LANES - ROWS * k, 1) for k in range(1, TOP_HITS)]
        best = parts if best is None else merged(best, parts)
    segment = lax.broadcasted_iota(jnp.int32, (blocks, LANES), 1) // ROWS
    final = jnp.zeros((blocks, LANES), jnp.float32)
    for k in range(TOP_HITS):
        moved = pltpu.roll(best[k], ROWS * k, 1) if k else best[k]
        final = jnp.where((segment == k) | (segment == TOP_HITS + k), moved, final)
    final = jnp.where(final <= 0.5 * EMPTY, floor_score, final * q_scale[...])
    fin[...] = final
    copies = [
        remote(fin, ybuf.at[y], y_send.at[step], y_recv.at[step], (m, turn(y, step, NY)))
        for step in range(1, NY)
    ]
    for copy in copies:
        copy.start()
    own = pltpu.make_async_copy(fin, ybuf.at[y], here_sem.at[NZ + 4])
    own.start()
    own.wait()
    for copy in copies:
        copy.wait()
    out[...] = ybuf[...]


def per_device(queries, query_mass, first_range, library, library_mass, shuffle):
    m = lax.axis_index("mass")
    y = lax.axis_index("sub")
    count, q_rows, depth = queries.shape
    lib_rows = library.shape[0]
    quarters = queries.reshape(count * NY, ROWS, depth)
    rows_z = jnp.arange(NZ, dtype=jnp.int32)[:, None, None] * (NX * NC)
    low = rows_z - 2 + 3 * jnp.arange(SLOTS, dtype=jnp.int32)[None, :, None]
    inside = (first_range >= low) & (first_range <= low + 2) & (first_range <= rows_z + 7)
    block_ids = jnp.arange(count, dtype=jnp.int32)
    chosen = jnp.sum(jnp.where(inside, block_ids, 0), axis=2).reshape(-1)
    send = jnp.take(quarters, chosen * NY + y, axis=0, mode="clip")

    own_mass = lax.dynamic_slice(query_mass, (0, y * ROWS), (count, ROWS))
    own_global = own_mass + first_range[:, None] * BINS
    ranges = jnp.arange(CHIPS * NC, dtype=jnp.int32)[:, None]
    covers = (first_range[None, :] <= ranges) & (ranges < first_range[None, :] + WINDOW)
    row_start = (ranges // 8) * 8
    pair = jnp.maximum((ranges % 8) // 2 - 1, 0)
    flag = (first_range[None, :] - row_start + 2) // 3 - pair
    code = (own_global[None, :, :] + int(OFFSET)) * 2 + flag[:, :, None]
    code = jnp.sum(jnp.where(covers[:, :, None], code, 0), axis=1).astype(jnp.float32)
    lane = jnp.arange(LANES, dtype=jnp.int32)
    msg = jnp.where(lane // ROWS == (m // NC) % 16, jnp.tile(code, (1, LANES // ROWS)), 0.0)
    msg = msg.reshape(CHIPS, NC, 1, LANES)

    own_rows = lax.dynamic_slice(queries, (0, y * ROWS, 0), (count, ROWS, depth)).astype(jnp.float32)
    q_scale = lax.rsqrt(jnp.sum(own_rows * own_rows, axis=2) + epsilon)
    q_scale = jnp.tile(q_scale, (1, LANES // ROWS))

    vmem = pl.BlockSpec(memory_space=pltpu.VMEM)
    f32, bf16 = jnp.float32, jnp.bfloat16
    dma = pltpu.SemaphoreType.DMA
    range_rows = NY * lib_rows
    found = pl.pallas_call(
        search_kernel,
        out_shape=jax.ShapeDtypeStruct((NY, count, LANES), f32),
        in_specs=[pl.BlockSpec(memory_space=pltpu.SMEM)] + [vmem] * 6,
        out_specs=vmem,
        scratch_shapes=[
            pltpu.VMEM((NZ, SLOTS, ROWS, depth), bf16),
            pltpu.VMEM((NZ, NX, 2, ROWS, depth), bf16),
            pltpu.VMEM((CHIPS, NC, 1, LANES), f32),
            pltpu.VMEM((NC, NY, lib_rows, depth), bf16),
            pltpu.VMEM((NC, NY, 1, LANES), f32),
            pltpu.VMEM((NC, range_rows, depth), bf16),
            pltpu.VMEM((depth, depth), bf16),
            pltpu.VMEM((CHIPS * ROWS, depth), bf16),
            pltpu.VMEM((NC, range_rows, LANES), f32),
            pltpu.VMEM((NC, range_rows, LANES), f32),
            pltpu.VMEM((range_rows, CHIPS * ROWS), f32),
            pltpu.VMEM((range_rows, CHIPS * ROWS), f32),
            pltpu.VMEM((CHIPS, NC, 1, LANES), f32),
            pltpu.VMEM((CHIPS * NC, 1, LANES), f32),
            pltpu.VMEM((WINDOW, count, LANES), f32),
            pltpu.VMEM((count, LANES), f32),
            pltpu.VMEM((NY, count, LANES), f32),
            dma((NZ,)), dma((NZ,)), dma((NZ, NX)), dma((NZ, NX)), dma, dma, dma, dma,
            dma((4,)), dma((4,)), dma((4,)), dma((4,)), dma((8,)), dma((8,)), dma((NY,)), dma((NY,)),
            dma((NZ + 5,)),
        ],
        compiler_params=pltpu.CompilerParams(collective_id=0, has_side_effects=True),
        name="search",
    )(
        first_range, send, msg, library, library_mass.astype(f32).reshape(1, LANES),
        shuffle.reshape(1, depth), q_scale,
    )
    found = found.reshape(NY, count, 16, ROWS)[:, :, :2 * TOP_HITS]
    found = jnp.transpose(found, (1, 2, 0, 3)).reshape(count, 2 * TOP_HITS, q_rows)
    return (found[:, :TOP_HITS], found[:, TOP_HITS:])


def solution(mesh):
    return jax.shard_map(
        per_device,
        mesh=mesh,
        in_specs=(
            P("mass", None, None),
            P("mass", None),
            P("mass"),
            P(("mass", "sub"), None),
            P(("mass", "sub")),
            P(),
        ),
        out_specs=(P("mass", None, None), P("mass", None, None)),
        check_vma=False,
    )
```

time: 560 us -> 69.1 us (0.12)
  other arithmetic: 381 us -> 7.77 us
  waiting for transfers between devices: 105 us -> 0 us
  Pallas kernels: 0 us -> 55.2 us
  starting transfers between devices: 44.6 us -> 0 us
  local copies, waits for them, and re-layouts: 20.4 us -> 5 us
  matrix products: 7.15 us -> 0 us
    top_k x2 -> x0, other arithmetic: 282 us -> none  [the longest x1 141 us: score_lanes(): target_lane = jnp.transpose(lax.top_k(target_score, TOP_HITS)[0], (0, 2, 1))]
    all_to_all x6 -> x0, waiting for transfers between devices: 105 us -> none  [the longest x1 89.5 us: per_device(): lax.all_to_all(outgoing, 'mass', split_axis=0, concat_axis=0, tiled=True)]
    sort x6 -> x0, other arithmetic: 84.1 us -> none  [best_of(): ordered = -jnp.sort(-values, axis=1)]
    pallas_call x0 -> x1, Pallas kernels: none -> 55.2 us  [per_device(): pl.pallas_call(search_kernel, out_shape=jax.ShapeDtypeStruct((NY, count,...]
    all_to_all x6 -> x0, starting transfers between devices: 44.6 us -> none  [the longest x1 13.3 us: per_device(): lax.all_to_all(outgoing, 'mass', split_axis=0, concat_axis=0, tiled=True)]
    gather x6 -> x1, local copies, waits for them, and re-layouts: 9.24 us -> 1.37 us  [per_device(): send = jnp.take(quarters, chosen * NY + y, axis=0, mode='clip')]
    dot_general x2 -> x0, matrix products: 7.15 us -> none  [the longest x1 3.59 us: score_lanes(): jnp.einsum('srd,ld->srl', query_rows, spectra, preferred_element_type=jnp...]
  transfers between devices with their start and end apart: 6 -> 0, of which waited for: 3 -> 0; matrix products, arithmetic and copies ran while one was open for 42% -> 0% of each run, Pallas kernels for 0% -> 0%
where the time goes in v1:
time: 69.1 us; the launch traced here: 68.7 us
  Pallas kernels  55.2 us (80%)
  other arithmetic  7.77 us (11%)
  local copies, waits for them, and re-layouts  5 us (7%)
  between operations  0.75 us (1%)
    pallas_call x1, Pallas kernels, per_device(): pl.pallas_call(search_kernel, out_shape=jax.ShapeDtypeStruct((NY, count,...  55.2 us
    unnamed x4, local copies, waits for them, and re-layouts  1.42 us

profile of v1, /device:TPU:1, one launch (start us, length us, event | category | flops | bytes accessed | tf_op | source)
XLA Modules:
  0.0 68.7 jit_solution(4727646476455891700)
XLA Ops:
  0.6 0.0 copy-start
  0.7 1.3 %convert_bitcast_fusion.lib_mass = f32[1,128]{1,0:T(1,128)} fusion(s32[128]{0:T(128)} %param.10), kind=kLoop, calls=%fused_computation.39 | loop fusion | flops 128 | bytes 1024 | tf_op jit(solution)/shard_map/reshape | solution.py:413
  2.0 0.7 %broadcast_compare_fusion = pred[8,16]{1,0:T(8,128)(4,1)S(1)} fusion(s32[16]{0:T(128)} %first_ref.1, s32[8]{0:T(128)S(1)} %fusion.5), kind=kLoop, calls=%fused_computation.21 | loop fusion | flops 128 | bytes 224 | tf_op jit(solution)/shard_map/le | solution.py:357
  2.7 0.7 broadcast_add_fusion.2
  3.4 0.7 %fusion.2 = pred[64,16]{0,1:T(8,128)(4,1)S(1)} fusion(s32[16]{0:T(128)S(1)} %get-tuple-element.14, s32[16]{0:T(128)} %first_ref.1), kind=kLoop, calls=%fused_computation.17 | loop fusion | flops 3072 | bytes 1152 | tf_op jit(solution)/shard_map/and | solution.py:365
  4.1 0.1 broadcast_add_fusion.1
  4.2 0.9 %select_reduce_fusion.1 = s32[8,4]{0,1:T(4,128)S(1)} fusion(s32[8,4]{0,1:T(4,128)S(1)} %get-tuple-element.13, s32[8,4]{0,1:T(4,128)S(1)} %get-tuple-element.12, s32[16]{0:T(128)} %first_ref.1, pred[8,16]{1,0:T(8,128)(4,1)S(1)} %broadcast_compare_fusion), kind=kLoop, calls=%fused_computation.7 | loop fusion | flops 3040 | bytes 576 | tf_op jit(solution)/shard_map/reduce_sum | solution.py:359
  5.1 0.1 copy.31
  5.2 0.1 reshape.358
  5.3 0.7 %fusion = s32[64,16]{0,1:T(8,128)S(1)} fusion(s32[64]{0:T(128)S(1)} %get-tuple-element.17, s32[64]{0:T(128)S(1)} %get-tuple-element.16, s32[16]{0:T(128)} %first_ref.1), kind=kLoop, calls=%fused_computation.9 | loop fusion | flops 11264 | bytes 4672 | tf_op jit(solution)/shard_map/sub | solution.py:368
  6.0 0.8 %add_multiply_fusion = s32[16,8]{1,0:T(8,128)S(1)} fusion(s32[16,32]{1,0:T(8,128)} %param.7, s32[]{:T(128)S(6)} %select_n.81, s32[16]{0:T(128)S(1)} %get-tuple-element.15), kind=kLoop, calls=%fused_computation.13 | loop fusion | flops 384 | bytes 1092 | tf_op jit(solution)/shard_map/mul | solution.py:369
  6.8 0.1 select_reduce_fusion
  6.9 1.1 %multiply_reduce_fusion = f32[16,8]{1,0:T(8,128)S(1)} fusion(bf16[16,32,1024]{2,1,0:T(8,128)(2,1)} %param.6, s32[]{:T(128)S(6)} %select_n.81), kind=kLoop, calls=%fused_computation.1 | loop fusion | flops 393088 | bytes 262660 | tf_op jit(solution)/shard_map/reduce_sum | solution.py:376
  8.0 0.1 copy.34
  8.1 0.1 copy.32
  8.2 0.7 copy.35.q_scale
  8.9 0.3 tile.9
  9.2 0.6 broadcast_select_fusion.msg
  9.8 0.0 copy-done
  9.8 1.4 %gather_fusion = bf16[32,8,1024]{2,1,0:T(8,128)(2,1)} fusion(bf16[64,8,1024]{2,1,0:T(8,128)(2,1)S(1)} %bitcast.14, s32[1024]{0:T(1024)S(1)} %pad_clamp_fusion), kind=kCustom, calls=%fused_computation | custom fusion | bytes 1048704 | tf_op jit(solution)/shard_map/jit(_take)/gather | solution.py:360
  11.2 55.2 %search.1 = f32[4,16,128]{2,1,0:T(8,128)} custom-call(s32[16]{0:T(128)} %first_ref.1, bf16[32,8,1024]{2,1,0:T(8,128)(2,1)} %gather_fusion, f32[32,2,1,128]{3,2,1,0:T(1,128)} %broadcast_select_fusion.msg, bf16[128,1024]{1,0:T(8,128)(2,1)} %lib.1, f32[1,128]{1,0:T(1,128)} %convert_bitcast_fusion.lib_mass, s32[1,1024]{1,0:T(1,128)} %bitcast.16, ...), custom_call_target="tpu_custom_call" | custom-call | tf_op jit(solution)/shard_map/search/pallas_call | solution.py:383
  66.4 0.9 %copy.36 = f32[4,16,128]{1,2,0:T(8,128)S(1)} copy(f32[4,16,128]{2,1,0:T(8,128)} %search.1) | data formatting | bytes 65536 | tf_op jit(solution)/shard_map/search/pallas_call | solution.py:383
  67.3 0.7 %copy.39 = f32[16,5,32]{2,0,1:T(8,128)} copy(f32[16,5,32]{0,2,1:T(8,128)S(1)} %get-tuple-element.10) | data formatting | bytes 20480
  68.0 0.7 %copy.38 = f32[16,5,32]{2,0,1:T(8,128)} copy(f32[16,5,32]{0,2,1:T(8,128)S(1)} %get-tuple-element.11) | data formatting | bytes 20480
  (13 shorter events, 0.1 us)
Async XLA Ops:
  0.6 9.2 %copy-start = (bf16[16,32,1024]{2,1,0:T(8,128)(2,1)S(1)}, bf16[16,32,1024]{2,1,0:T(8,128)(2,1)}, u32[]{:S(2)}) copy-start(bf16[16,32,1024]{2,1,0:T(8,128)(2,1)} %param.6) | copy-start | bytes 3145732

commit v2 on v1

v2 whole, which is shorter than its diff:
```python
import jax
import jax.numpy as jnp
from jax import lax
from jax.experimental import pallas as pl
from jax.experimental.pallas import tpu as pltpu
from jax.sharding import PartitionSpec as P

BINS = 16
TOLERANCE = 4
WINDOW = 3
TOP_HITS = 5
NZ, NX, NC, NY = 8, 4, 2, 4
CHIPS = NZ * NX
SLOTS = 4
ROWS = 8
LANES = 128
OFFSET = 64.0
epsilon = 1e-06
floor_score = -3.0
EMPTY = -1e30
MESH = pl.DeviceIdType.MESH
ORDER = (0, 1, 7, 2, 6, 3, 5, 4)


def insert(best, new, start=0):
    best = list(best)
    for k in range(start, TOP_HITS):
        high = jnp.maximum(best[k], new)
        if k + 1 < TOP_HITS:
            new = jnp.minimum(best[k], new)
        best[k] = high
    return best


def merged(former, latter):
    for k in range(TOP_HITS):
        former = insert(former, latter[k], k)
    return former


def spread(rows):
    for shift in (8, 16, 32, 64):
        rows = rows + pltpu.roll(rows, shift, 1)
    return rows


def swap_blocks(table):
    row = lax.broadcasted_iota(jnp.int32, table.shape, 0)
    segment = lax.broadcasted_iota(jnp.int32, table.shape, 1) // ROWS
    for bit in range(4):
        step = 1 << bit
        up = pltpu.roll(pltpu.roll(table, 16 - step, 0), ROWS * step, 1)
        down = pltpu.roll(pltpu.roll(table, step, 0), LANES - ROWS * step, 1)
        row_bit = (row // step) % 2
        segment_bit = (segment // step) % 2
        table = jnp.where(row_bit == segment_bit, table, jnp.where(row_bit == 0, up, down))
    return table


def search_kernel(
    first_ref, queries, q_mass, lib, lib_mass, shuffle, out,
    qown, send, code, zbuf, zcode, qbuf, xcode, lmbuf, spectra, onehot, qsel, scale_rep, mass_rep,
    flags, scores, obuf, rbuf, abuf, norms, fin, ybuf,
    z_send, z_recv, zc_send, zc_recv, x_send, x_recv, xc_send, xc_recv, r_send, r_recv,
    l_send, l_recv, c_send, c_recv, lm_send, lm_recv, y_send, y_recv, here_sem,
):
    m = lax.axis_index("mass")
    y = lax.axis_index("sub")
    blocks = q_mass.shape[0]
    lib_rows, depth = lib.shape
    range_rows = NY * lib_rows
    z = m // (NX * NC)
    x = (m // NC) % NX
    c = m % NC
    g = m // NC
    partner = m + 1 - 2 * c

    def device(chip):
        return (chip * NC + c, y)

    def turn(value, step, count):
        return lax.rem(value + step, count)

    def remote(src, dst, send_sem, recv_sem, target):
        return pltpu.make_async_remote_copy(
            src_ref=src, dst_ref=dst, send_sem=send_sem, recv_sem=recv_sem,
            device_id=target, device_id_type=MESH,
        )

    barrier = pltpu.get_barrier_semaphore()
    peers = [device(turn(z, s, NZ) * NX + x) for s in range(1, NZ)]
    peers += [device(z * NX + turn(x, s, NX)) for s in range(1, NX)]
    peers += [(m, turn(y, s, NY)) for s in range(1, NY)]
    peers += [(partner, turn(y, s, NY)) for s in range(NY)]
    for peer in peers:
        pl.semaphore_signal(barrier, inc=1, device_id=peer, device_id_type=MESH)

    take_queries = pltpu.make_async_copy(queries.at[:, y], qown, here_sem.at[0])
    take_queries.start()
    own_lib = spectra.at[c, 0, pl.ds(y * lib_rows, lib_rows)]
    take_lib = pltpu.make_async_copy(lib, own_lib, here_sem.at[1])
    take_lib.start()
    take_mass = pltpu.make_async_copy(lib_mass, lmbuf.at[c, y], here_sem.at[2])
    take_mass.start()

    lane = lax.broadcasted_iota(jnp.int32, (ROWS, LANES), 1)
    row8 = lax.broadcasted_iota(jnp.int32, (ROWS, LANES), 0)
    wide_lane = lax.broadcasted_iota(jnp.int32, (blocks, LANES), 1)
    own_mass = jnp.concatenate(
        [q_mass[...].astype(jnp.float32), jnp.zeros((blocks, LANES - NY * ROWS), jnp.float32)], axis=1
    )
    own_mass = pltpu.roll(own_mass, turn(LANES - y * ROWS, 0, LANES), 1)
    own_mass = spread(jnp.where(wide_lane < ROWS, own_mass, 0.0))
    pair_start = jnp.maximum(row8 // 2 - 1, 0)
    for at, dz in enumerate(ORDER):
        base = turn(z, dz, NZ) * (NX * NC)
        ranges = row8 + base
        threshold = base + 3 * pair_start + 1
        tile = jnp.zeros((ROWS, LANES), jnp.float32)
        for b in range(blocks):
            start = first_ref[b]
            shift = ((start - base) * BINS).astype(jnp.float32) + OFFSET
            value = own_mass[b:b + 1, :] + shift
            value = jnp.where(start >= threshold, -value, value)
            ahead = ranges - start
            tile = jnp.where((ahead >= 0) & (ahead < WINDOW), value, tile)
        dx = lax.rem(row8 // 2 - x + NX, NX)
        place = lax.rem(at * NX + dx, 16)
        code[at] = jnp.where(lane // ROWS == place, tile, 0.0).astype(jnp.bfloat16)

    take_queries.wait()

    def gather(i, carry):
        row = i // SLOTS
        low = row * (NX * NC) - 2 + 3 * (i % SLOTS)
        high = jnp.minimum(low + 2, row * (NX * NC) + NX * NC - 1)
        chosen = jnp.int32(0)
        for b in range(blocks):
            start = first_ref[b]
            chosen = jnp.where((start >= low) & (start <= high), b, chosen)
        send[i] = qown[chosen]
        return carry

    lax.fori_loop(0, NZ * SLOTS, gather, 0)
    take_lib.wait()
    take_mass.wait()

    pl.semaphore_wait(barrier, len(peers))

    def z_copies(at):
        zt = turn(z, ORDER[at], NZ)
        target = device(zt * NX + x)
        return (
            remote(send.at[pl.ds(zt * SLOTS, SLOTS)], zbuf.at[at], z_send.at[at], z_recv.at[at], target),
            remote(code.at[at], zcode.at[at], zc_send.at[at], zc_recv.at[at], target),
        )

    def x_copies(at, dx):
        xt = turn(x, dx, NX)
        start = jnp.maximum(xt - 1, 0)
        if at:
            pair, codes = zbuf.at[at, pl.ds(start, 2)], zcode.at[at]
        else:
            pair, codes = send.at[pl.ds(z * SLOTS + start, 2)], code.at[0]
        to_pair, to_codes = qbuf.at[at, dx], xcode.at[at, dx]
        if dx == 0:
            return (
                pltpu.make_async_copy(pair, to_pair, here_sem.at[3 + at]),
                pltpu.make_async_copy(codes, to_codes, here_sem.at[3 + NZ + at]),
            )
        target = device(z * NX + xt)
        return (
            remote(pair, to_pair, x_send.at[at, dx], x_recv.at[at, dx], target),
            remote(codes, to_codes, xc_send.at[at, dx], xc_recv.at[at, dx], target),
        )

    def start(copies):
        for copy in copies:
            copy.start()

    def forward(at):
        for dx in (2, 1, 3, 0):
            start(x_copies(at, dx))

    for at in range(1, NZ):
        start(z_copies(at))
    forward(0)

    half = lib_rows // 2
    up, down, opposite = turn(y, 1, NY), turn(y, NY - 1, NY), turn(y, 2, NY)

    def piece(at, first=0, count=lib_rows):
        return spectra.at[c, 0, pl.ds(at * lib_rows + first, count)]

    def piece_copy(part, sems, at, target):
        return remote(part, part, sems[0].at[at], sems[1].at[at], target)

    l_sems, c_sems = (l_send, l_recv), (c_send, c_recv)
    own_up = piece_copy(piece(y), l_sems, 0, (m, up))
    own_down = piece_copy(piece(y), l_sems, 1, (m, down))
    own_core = piece_copy(piece(y), c_sems, 0, (partner, y))
    start((own_up, own_down, own_core))
    lm_copies = []
    for core in range(NC):
        for step in range(NY):
            if core or step:
                at = core * NY + step
                target = (partner if core else m, turn(y, step, NY))
                lm_copies.append(remote(
                    lmbuf.at[c, y], lmbuf.at[c, y], lm_send.at[at], lm_recv.at[at], target
                ))
    start(lm_copies)

    chunk = 64
    names = shuffle[...]

    def build(i, carry):
        base = pl.multiple_of(i * chunk, chunk)
        index = lax.broadcasted_iota(jnp.int32, (chunk, depth), 0) + base
        onehot[pl.ds(base, chunk), :] = jnp.where(index == names, 1.0, 0.0).astype(jnp.bfloat16)
        return carry

    lax.fori_loop(0, depth // chunk, build, 0)

    def prepare(e, at):
        base = pl.multiple_of(at * lib_rows, lib_rows)
        rows = spectra[e, 0, pl.ds(base, lib_rows), :]
        wide = rows.astype(jnp.float32)
        total = jnp.sum(wide * wide, axis=1, keepdims=True)
        scale_rep[e, pl.ds(base, lib_rows), :] = jnp.broadcast_to(
            lax.rsqrt(total + epsilon), (lib_rows, LANES)
        )
        spectra[e, 1, pl.ds(base, lib_rows), :] = jnp.dot(
            rows, onehot[...], preferred_element_type=jnp.float32
        ).astype(jnp.bfloat16)

    def arrive(at):
        for copy in z_copies(at):
            copy.wait_recv()
        forward(at)

    arrive(1)
    arrive(2)
    prepare(c, y)
    arrive(3)
    arrive(4)

    def norm(i, carry):
        wide = qown[pl.ds(i * 2, 2)].astype(jnp.float32).reshape(2 * ROWS, depth)
        total = jnp.sum(wide * wide, axis=1, keepdims=True)
        norms[pl.ds(pl.multiple_of(i * 16, 16), 16), :] = jnp.broadcast_to(
            lax.rsqrt(total + epsilon), (2 * ROWS, LANES)
        )
        return carry

    lax.fori_loop(0, blocks // 2, norm, 0)

    own_up.wait_recv()
    relay_up = piece_copy(piece(down, 0, half), l_sems, 2, (m, up))
    core_down = piece_copy(piece(down), c_sems, 1, (partner, y))
    start((relay_up, core_down))
    own_down.wait_recv()
    relay_down = piece_copy(piece(up, half, half), l_sems, 3, (m, down))
    core_up = piece_copy(piece(up), c_sems, 2, (partner, y))
    start((relay_down, core_up))
    arrive(5)
    own_core.wait_recv()
    prepare(1 - c, y)
    prepare(c, down)
    arrive(6)
    prepare(c, up)
    core_down.wait_recv()
    prepare(1 - c, down)
    arrive(7)
    core_up.wait_recv()
    prepare(1 - c, up)
    relay_up.wait_recv()
    relay_down.wait_recv()
    core_opposite = piece_copy(piece(opposite), c_sems, 3, (partner, y))
    core_opposite.start()
    prepare(c, opposite)

    for copy in lm_copies:
        copy.wait()
    for e in range(NC):
        for at in range(NY):
            mass = jnp.broadcast_to(lmbuf[e, at].astype(jnp.float32), (lib_rows, LANES)).T
            mass = mass + ((x * NC + e) * BINS).astype(jnp.float32) + OFFSET
            mass_rep[e, at * lib_rows:(at + 1) * lib_rows, :] = mass
    core_opposite.wait_recv()
    prepare(1 - c, opposite)

    tables = [[None, None], [None, None]]
    for lg in range(2):
        first_at = lg * NZ // 2
        combined = jnp.zeros((ROWS, LANES), jnp.float32)
        for at in range(first_at, first_at + NZ // 2):
            for dx in range(NX):
                for copy in x_copies(at, dx):
                    if dx:
                        copy.wait_recv()
                    else:
                        copy.wait()
                tile = xcode[at, dx].astype(jnp.float32)
                combined = combined + jnp.abs(tile)
                flags[at * NX + dx] = jnp.broadcast_to(
                    jnp.sum(tile, axis=1, keepdims=True), (ROWS, LANES)
                )

        def choose(i, carry):
            at = first_at + i // 2
            side = (i % 2) * 2
            first = qbuf[at, pl.ds(side, 2), 0].astype(jnp.float32)
            second = qbuf[at, pl.ds(side, 2), 1].astype(jnp.float32)
            base = pl.multiple_of(i * 16, 16)
            for e in range(NC):
                flag = flags[pl.ds(at * NX + side, 2), pl.ds(x * NC + e, 1), :][:, :, :1]
                picked = jnp.where(flag < 0.0, second, first)
                qsel[e, pl.ds(base, 16), :] = picked.reshape(2 * ROWS, depth).astype(jnp.bfloat16)
            return carry

        lax.fori_loop(0, NZ, choose, 0)

        masses = []
        for e in range(NC):
            scores[e] = lax.dot_general(
                spectra[e].reshape(2 * range_rows, depth), qsel[e], (((1,), (1,)), ((), ())),
                preferred_element_type=jnp.float32,
            )
            code_row = jnp.sum(jnp.where(row8 == x * NC + e, combined, 0.0), axis=0, keepdims=True)
            masses.append(jnp.broadcast_to(code_row, (ROWS, LANES)))

        def scan(i, best):
            base = pl.multiple_of(i * ROWS, ROWS)
            found = []
            for e in range(NC):
                scale = scale_rep[e, pl.ds(base, ROWS), :]
                allowed = jnp.abs(masses[e] - mass_rep[e, pl.ds(base, ROWS), :]) <= TOLERANCE
                for kind in range(2):
                    score = scores[e, pl.ds(kind * range_rows + base, ROWS), :] * scale
                    at = (e * 2 + kind) * TOP_HITS
                    found += insert(best[at:at + TOP_HITS], jnp.where(allowed, score, EMPTY))
            return tuple(found)

        nothing = jnp.full((ROWS, LANES), EMPTY, jnp.float32)
        best = lax.fori_loop(
            0, range_rows // ROWS, scan, (nothing,) * (4 * TOP_HITS), unroll=2
        )
        for e in range(NC):
            lanes = []
            for kind in range(2):
                at = (e * 2 + kind) * TOP_HITS
                part = list(best[at:at + TOP_HITS])
                for shift in (4, 2, 1):
                    part = merged(part, [pltpu.roll(v, shift, 0) for v in part])
                lanes += part
            upper = lanes[0]
            for k in range(1, 8):
                upper = jnp.where(row8 == k, lanes[k], upper)
            lower = jnp.where(row8 == 0, lanes[8], lanes[9])
            table = swap_blocks(jnp.concatenate([upper, lower], axis=0))
            for k in range(16):
                obuf[lg * 16 + k, e] = table[k:k + 1, :]

    for at in range(NZ):
        for dx in range(NX):
            if at or dx:
                chip = turn(z, NZ - ORDER[at], NZ) * NX + turn(x, NX - dx, NX)
                remote(
                    obuf.at[at * NX + dx], rbuf.at[pl.ds(g * NC, NC)], r_send, r_recv, device(chip)
                ).start()
    keep = pltpu.make_async_copy(obuf.at[0], rbuf.at[pl.ds(g * NC, NC)], here_sem.at[0])
    keep.start()

    for at in range(NZ):
        if at:
            for copy in z_copies(at):
                copy.wait_send()
        for dx in range(1, NX):
            for copy in x_copies(at, dx):
                copy.wait_send()
    for copy in (own_up, own_down, relay_up, relay_down, own_core, core_down, core_up, core_opposite):
        copy.wait_send()

    block_row = lax.broadcasted_iota(jnp.int32, (blocks, LANES), 0)
    q_scale = spread(jnp.where(wide_lane // ROWS == block_row, norms[...].T[:blocks], 0.0))

    keep.wait()
    for sem in (r_send, r_recv):
        others = rbuf.at[pl.ds(0, NC * (CHIPS - 1))]
        pltpu.make_async_copy(others, others, sem).wait()

    for b in range(blocks):
        first = first_ref[b]
        for w in range(WINDOW):
            abuf[w, b:b + 1, :] = rbuf[first + w]
    best = None
    for w in range(WINDOW):
        rows = abuf[w]
        parts = [rows] + [pltpu.roll(rows, LANES - ROWS * k, 1) for k in range(1, TOP_HITS)]
        best = parts if best is None else merged(best, parts)
    segment = wide_lane // ROWS
    final = jnp.zeros((blocks, LANES), jnp.float32)
    for k in range(TOP_HITS):
        moved = pltpu.roll(best[k], ROWS * k, 1) if k else best[k]
        final = jnp.where((segment == k) | (segment == TOP_HITS + k), moved, final)
    fin[...] = jnp.where(final <= 0.5 * EMPTY, floor_score, final * q_scale)
    copies = [
        remote(fin, ybuf.at[y], y_send.at[step], y_recv.at[step], (m, turn(y, step, NY)))
        for step in range(1, NY)
    ]
    start(copies)
    own = pltpu.make_async_copy(fin, ybuf.at[y], here_sem.at[1])
    own.start()
    own.wait()
    for copy in copies:
        copy.wait()
    out[...] = ybuf[...]


def per_device(queries, query_mass, first_range, library, library_mass, shuffle):
    count, q_rows, depth = queries.shape
    lib_rows = library.shape[0]
    f32, bf16 = jnp.float32, jnp.bfloat16
    vmem = pl.BlockSpec(memory_space=pltpu.VMEM)
    smem = pl.BlockSpec(memory_space=pltpu.SMEM)
    hbm = pl.BlockSpec(memory_space=pl.ANY)
    dma = pltpu.SemaphoreType.DMA
    range_rows = NY * lib_rows
    found = pl.pallas_call(
        search_kernel,
        out_shape=jax.ShapeDtypeStruct((NY, count, LANES), f32),
        in_specs=[smem, hbm, vmem, hbm, hbm, vmem],
        out_specs=vmem,
        scratch_shapes=[
            pltpu.VMEM((count, ROWS, depth), bf16),
            pltpu.VMEM((NZ * SLOTS, ROWS, depth), bf16),
            pltpu.VMEM((NZ, ROWS, LANES), bf16),
            pltpu.VMEM((NZ, SLOTS, ROWS, depth), bf16),
            pltpu.VMEM((NZ, ROWS, LANES), bf16),
            pltpu.VMEM((NZ, NX, 2, ROWS, depth), bf16),
            pltpu.VMEM((NZ, NX, ROWS, LANES), bf16),
            pltpu.VMEM((NC, NY, 1, LANES), jnp.int32),
            pltpu.VMEM((NC, 2, range_rows, depth), bf16),
            pltpu.VMEM((depth, depth), bf16),
            pltpu.VMEM((NC, LANES, depth), bf16),
            pltpu.VMEM((NC, range_rows, LANES), f32),
            pltpu.VMEM((NC, range_rows, LANES), f32),
            pltpu.VMEM((CHIPS, ROWS, LANES), f32),
            pltpu.VMEM((NC, 2 * range_rows, LANES), f32),
            pltpu.VMEM((CHIPS, NC, 1, LANES), f32),
            pltpu.VMEM((CHIPS * NC, 1, LANES), f32),
            pltpu.VMEM((WINDOW, count, LANES), f32),
            pltpu.VMEM((count * ROWS, LANES), f32),
            pltpu.VMEM((count, LANES), f32),
            pltpu.VMEM((NY, count, LANES), f32),
            dma((NZ,)), dma((NZ,)), dma((NZ,)), dma((NZ,)),
            dma((NZ, NX)), dma((NZ, NX)), dma((NZ, NX)), dma((NZ, NX)), dma, dma,
            dma((4,)), dma((4,)), dma((4,)), dma((4,)), dma((8,)), dma((8,)), dma((NY,)), dma((NY,)),
            dma((3 + 2 * NZ,)),
        ],
        compiler_params=pltpu.CompilerParams(collective_id=0, has_side_effects=True),
        name="search",
    )(
        first_range, queries.reshape(count, NY, ROWS, depth), query_mass, library,
        library_mass.reshape(1, LANES), shuffle.reshape(1, depth),
    )
    found = found.reshape(NY, count, 16, ROWS)[:, :, :2 * TOP_HITS]
    found = jnp.transpose(found, (1, 2, 0, 3)).reshape(count, 2 * TOP_HITS, q_rows)
    return (found[:, :TOP_HITS], found[:, TOP_HITS:])


def solution(mesh):
    return jax.shard_map(
        per_device,
        mesh=mesh,
        in_specs=(
            P("mass", None, None),
            P("mass", None),
            P("mass"),
            P(("mass", "sub"), None),
            P(("mass", "sub")),
            P(),
        ),
        out_specs=(P("mass", None, None), P("mass", None, None)),
        check_vma=False,
    )
```

time: 69.1 us -> 51.4 us (0.74)
  other arithmetic: 7.77 us -> 0 us
  Pallas kernels: 55.2 us -> 48.2 us
  local copies, waits for them, and re-layouts: 5 us -> 2.31 us
    pallas_call x1, Pallas kernels: 55.2 us -> 48.2 us  [per_device(): pl.pallas_call(search_kernel, out_shape=jax.ShapeDtypeStruct((NY, count,...]
    reduce_sum x3 -> x0, other arithmetic: 2.05 us -> none  [the longest x1 1.09 us: per_device(): q_scale = lax.rsqrt(jnp.sum(own_rows * own_rows, axis=2) + epsilon)]
    gather x1 -> x0, local copies, waits for them, and re-layouts: 1.37 us -> none  [per_device(): send = jnp.take(quarters, chosen * NY + y, axis=0, mode='clip')]
    reshape x1 -> x0, other arithmetic: 1.32 us -> none  [per_device(): library_mass.astype(f32).reshape(1, LANES)]
    another operation x4 -> x0, local copies, waits for them, and re-layouts: 1 us -> none  [the longest x2 0.67 us: per_device(): q_scale = jnp.tile(q_scale, (1, LANES // ROWS))]
    mul x3 -> x0, other arithmetic: 0.79 us -> none  [the longest x1 0.78 us: per_device(): code = (own_global[None, :, :] + int(OFFSET)) * 2 + flag[:, :, None]]
    sub x2 -> x0, other arithmetic: 0.75 us -> none  [the longest x1 0.74 us: per_device(): flag = (first_range[None, :] - row_start + 2) // 3 - pair]
    add x4 -> x0, other arithmetic: 0.74 us -> none  [the longest x1 0.66 us: per_device(): first_range[None, :] + WINDOW]
where the time goes in v2:
time: 51.4 us; the launch traced here: 51.2 us
  Pallas kernels  48.2 us (94%)
  local copies, waits for them, and re-layouts  2.31 us (4%)
  between operations  0.66 us (1%)
    pallas_call x1, Pallas kernels, per_device(): pl.pallas_call(search_kernel, out_shape=jax.ShapeDtypeStruct((NY, count,...  48.2 us
    unnamed x2, local copies, waits for them, and re-layouts  1.41 us

profile of v2, /device:TPU:1, one launch (start us, length us, event | category | flops | bytes accessed | tf_op | source)
XLA Modules:
  0.0 51.2 jit_solution(12714227759936075171)
XLA Ops:
  0.6 48.2 %search.1 = f32[4,16,128]{2,1,0:T(8,128)} custom-call(s32[16]{0:T(128)} %first_ref.1, bf16[16,4,8,1024]{3,2,1,0:T(8,128)(2,1)} %bitcast.9, s32[16,32]{1,0:T(8,128)} %q_mass.1, bf16[128,1024]{1,0:T(8,128)(2,1)} %lib.1, s32[1,128]{1,0:T(1,128)} %bitcast.12, s32[1,1024]{1,0:T(1,128)} %bitcast.11), custom_call_target="tpu_custom_call" | custom-call | tf_op jit(solution)/shard_map/search/pallas_call | solution.py:430
  48.8 0.9 %copy.9 = f32[4,16,128]{1,2,0:T(8,128)S(1)} copy(f32[4,16,128]{2,1,0:T(8,128)} %search.1) | data formatting | bytes 65536 | tf_op jit(solution)/shard_map/search/pallas_call | solution.py:430
  49.8 0.7 %copy.12 = f32[16,5,32]{2,0,1:T(8,128)} copy(f32[16,5,32]{0,2,1:T(8,128)S(1)} %get-tuple-element.4) | data formatting | bytes 20480
  50.5 0.7 %copy.11 = f32[16,5,32]{2,0,1:T(8,128)} copy(f32[16,5,32]{0,2,1:T(8,128)S(1)} %get-tuple-element.5) | data formatting | bytes 20480
  (2 shorter events, 0.0 us)

commit v3 on v2

--- a/solution.py
+++ b/solution.py
@@ -58,11 +58,11 @@
 
 
 def search_kernel(
-    first_ref, queries, q_mass, lib, lib_mass, shuffle, out,
-    qown, send, code, zbuf, zcode, qbuf, xcode, lmbuf, spectra, onehot, qsel, scale_rep, mass_rep,
-    flags, scores, obuf, rbuf, abuf, norms, fin, ybuf,
+    first_ref, queries, q_mass, lib, lib_mass, shuffle, out_t, out_d,
+    qall, send, code, zbuf, zcode, qbuf, xcode, lmbuf, spectra, onehot, columns, scale_rep, mass_rep,
+    scores, obuf, rbuf, abuf, norms, q_scale,
     z_send, z_recv, zc_send, zc_recv, x_send, x_recv, xc_send, xc_recv, r_send, r_recv,
-    l_send, l_recv, c_send, c_recv, lm_send, lm_recv, y_send, y_recv, here_sem,
+    l_send, l_recv, c_send, c_recv, lm_send, lm_recv, here_sem,
 ):
     m = lax.axis_index("mass")
     y = lax.axis_index("sub")
@@ -95,7 +95,7 @@
     for peer in peers:
         pl.semaphore_signal(barrier, inc=1, device_id=peer, device_id_type=MESH)
 
-    take_queries = pltpu.make_async_copy(queries.at[:, y], qown, here_sem.at[0])
+    take_queries = pltpu.make_async_copy(queries, qall, here_sem.at[0])
     take_queries.start()
     own_lib = spectra.at[c, 0, pl.ds(y * lib_rows, lib_rows)]
     take_lib = pltpu.make_async_copy(lib, own_lib, here_sem.at[1])
@@ -138,7 +138,7 @@
         for b in range(blocks):
             start = first_ref[b]
             chosen = jnp.where((start >= low) & (start <= high), b, chosen)
-        send[i] = qown[chosen]
+        send[i] = qall[chosen, y]
         return carry
 
     lax.fori_loop(0, NZ * SLOTS, gather, 0)
@@ -245,15 +245,22 @@
     arrive(3)
     arrive(4)
 
+    wide_row = lax.broadcasted_iota(jnp.int32, (blocks, LANES), 0)
+
     def norm(i, carry):
-        wide = qown[pl.ds(i * 2, 2)].astype(jnp.float32).reshape(2 * ROWS, depth)
+        part, b = i // (blocks // 2), (i % (blocks // 2)) * 2
+        wide = qall[pl.ds(b, 2), part].astype(jnp.float32).reshape(2 * ROWS, depth)
         total = jnp.sum(wide * wide, axis=1, keepdims=True)
-        norms[pl.ds(pl.multiple_of(i * 16, 16), 16), :] = jnp.broadcast_to(
+        norms[part, pl.ds(pl.multiple_of(b * ROWS, 16), 16), :] = jnp.broadcast_to(
             lax.rsqrt(total + epsilon), (2 * ROWS, LANES)
         )
         return carry
 
-    lax.fori_loop(0, blocks // 2, norm, 0)
+    lax.fori_loop(0, NY * blocks // 2, norm, 0)
+    for part in range(NY):
+        q_scale[part * blocks:(part + 1) * blocks, :] = spread(
+            jnp.where(wide_lane // ROWS == wide_row, norms[part].T[:blocks], 0.0)
+        )
 
     own_up.wait_recv()
     relay_up = piece_copy(piece(down, 0, half), l_sems, 2, (m, up))
@@ -290,45 +297,40 @@
     core_opposite.wait_recv()
     prepare(1 - c, opposite)
 
-    tables = [[None, None], [None, None]]
+    def pack(at):
+        for dx in range(NX):
+            for copy in x_copies(at, dx):
+                if dx:
+                    copy.wait_recv()
+                else:
+                    copy.wait()
+        for slot in range(2):
+            for side in range(0, NX, 2):
+                rows = qbuf[at, side:side + 2, slot].astype(jnp.float32).reshape(2 * ROWS, depth)
+                base = slot * LANES + ((at * NX + side) % 16) * ROWS
+                columns[base:base + 16, :] = rows.astype(jnp.bfloat16)
+        tile = xcode[at, 0].astype(jnp.float32)
+        for dx in range(1, NX):
+            tile = tile + xcode[at, dx].astype(jnp.float32)
+        return tile
+
     for lg in range(2):
         first_at = lg * NZ // 2
-        combined = jnp.zeros((ROWS, LANES), jnp.float32)
-        for at in range(first_at, first_at + NZ // 2):
-            for dx in range(NX):
-                for copy in x_copies(at, dx):
-                    if dx:
-                        copy.wait_recv()
-                    else:
-                        copy.wait()
-                tile = xcode[at, dx].astype(jnp.float32)
-                combined = combined + jnp.abs(tile)
-                flags[at * NX + dx] = jnp.broadcast_to(
-                    jnp.sum(tile, axis=1, keepdims=True), (ROWS, LANES)
-                )
-
-        def choose(i, carry):
-            at = first_at + i // 2
-            side = (i % 2) * 2
-            first = qbuf[at, pl.ds(side, 2), 0].astype(jnp.float32)
-            second = qbuf[at, pl.ds(side, 2), 1].astype(jnp.float32)
-            base = pl.multiple_of(i * 16, 16)
-            for e in range(NC):
-                flag = flags[pl.ds(at * NX + side, 2), pl.ds(x * NC + e, 1), :][:, :, :1]
-                picked = jnp.where(flag < 0.0, second, first)
-                qsel[e, pl.ds(base, 16), :] = picked.reshape(2 * ROWS, depth).astype(jnp.bfloat16)
-            return carry
-
-        lax.fori_loop(0, NZ, choose, 0)
+        combined = pack(first_at)
+        for at in range(first_at + 1, first_at + NZ // 2):
+            combined = combined + pack(at)
 
         masses = []
+        others = []
         for e in range(NC):
             scores[e] = lax.dot_general(
-                spectra[e].reshape(2 * range_rows, depth), qsel[e], (((1,), (1,)), ((), ())),
+                spectra[e].reshape(2 * range_rows, depth), columns[...], (((1,), (1,)), ((), ())),
                 preferred_element_type=jnp.float32,
             )
             code_row = jnp.sum(jnp.where(row8 == x * NC + e, combined, 0.0), axis=0, keepdims=True)
-            masses.append(jnp.broadcast_to(code_row, (ROWS, LANES)))
+            code_row = jnp.broadcast_to(code_row, (ROWS, LANES))
+            masses.append(jnp.abs(code_row))
+            others.append(code_row < 0.0)
 
         def scan(i, best):
             base = pl.multiple_of(i * ROWS, ROWS)
@@ -337,7 +339,8 @@
                 scale = scale_rep[e, pl.ds(base, ROWS), :]
                 allowed = jnp.abs(masses[e] - mass_rep[e, pl.ds(base, ROWS), :]) <= TOLERANCE
                 for kind in range(2):
-                    score = scores[e, pl.ds(kind * range_rows + base, ROWS), :] * scale
+                    rows = pl.ds(kind * range_rows + base, ROWS)
+                    score = jnp.where(others[e], scores[e, rows, LANES:], scores[e, rows, :LANES]) * scale
                     at = (e * 2 + kind) * TOP_HITS
                     found += insert(best[at:at + TOP_HITS], jnp.where(allowed, score, EMPTY))
             return tuple(found)
@@ -362,14 +365,17 @@
             for k in range(16):
                 obuf[lg * 16 + k, e] = table[k:k + 1, :]
 
-    for at in range(NZ):
+    own_rows = (y * CHIPS + g) * NC
+    for at in range(NZ - 1, -1, -1):
         for dx in range(NX):
-            if at or dx:
-                chip = turn(z, NZ - ORDER[at], NZ) * NX + turn(x, NX - dx, NX)
-                remote(
-                    obuf.at[at * NX + dx], rbuf.at[pl.ds(g * NC, NC)], r_send, r_recv, device(chip)
-                ).start()
-    keep = pltpu.make_async_copy(obuf.at[0], rbuf.at[pl.ds(g * NC, NC)], here_sem.at[0])
+            chip = turn(z, NZ - ORDER[at], NZ) * NX + turn(x, NX - dx, NX)
+            for step in (2, 1, 3, 0):
+                if at or dx or step:
+                    remote(
+                        obuf.at[at * NX + dx], rbuf.at[pl.ds(own_rows, NC)], r_send, r_recv,
+                        (chip * NC + c, turn(y, step, NY)),
+                    ).start()
+    keep = pltpu.make_async_copy(obuf.at[0], rbuf.at[pl.ds(own_rows, NC)], here_sem.at[0])
     keep.start()
 
     for at in range(NZ):
@@ -382,40 +388,34 @@
     for copy in (own_up, own_down, relay_up, relay_down, own_core, core_down, core_up, core_opposite):
         copy.wait_send()
 
-    block_row = lax.broadcasted_iota(jnp.int32, (blocks, LANES), 0)
-    q_scale = spread(jnp.where(wide_lane // ROWS == block_row, norms[...].T[:blocks], 0.0))
-
     keep.wait()
     for sem in (r_send, r_recv):
-        others = rbuf.at[pl.ds(0, NC * (CHIPS - 1))]
+        others = rbuf.at[pl.ds(0, NC * (NY * CHIPS - 1))]
         pltpu.make_async_copy(others, others, sem).wait()
 
     for b in range(blocks):
         first = first_ref[b]
-        for w in range(WINDOW):
-            abuf[w, b:b + 1, :] = rbuf[first + w]
+        for part in range(NY):
+            for w in range(WINDOW):
+                row = part * blocks + b
+                abuf[w, row:row + 1, :] = rbuf[part * CHIPS * NC + first + w]
     best = None
     for w in range(WINDOW):
         rows = abuf[w]
         parts = [rows] + [pltpu.roll(rows, LANES - ROWS * k, 1) for k in range(1, TOP_HITS)]
         best = parts if best is None else merged(best, parts)
+    scale = q_scale[...]
     segment = wide_lane // ROWS
-    final = jnp.zeros((blocks, LANES), jnp.float32)
     for k in range(TOP_HITS):
-        moved = pltpu.roll(best[k], ROWS * k, 1) if k else best[k]
-        final = jnp.where((segment == k) | (segment == TOP_HITS + k), moved, final)
-    fin[...] = jnp.where(final <= 0.5 * EMPTY, floor_score, final * q_scale)
-    copies = [
-        remote(fin, ybuf.at[y], y_send.at[step], y_recv.at[step], (m, turn(y, step, NY)))
-        for step in range(1, NY)
-    ]
-    start(copies)
-    own = pltpu.make_async_copy(fin, ybuf.at[y], here_sem.at[1])
-    own.start()
-    own.wait()
-    for copy in copies:
-        copy.wait()
-    out[...] = ybuf[...]
+        value = jnp.where(best[k] <= 0.5 * EMPTY, floor_score, best[k] * scale)
+        for out, kind in ((out_t, 0), (out_d, TOP_HITS)):
+            row = jnp.zeros((blocks, LANES), jnp.float32)
+            for part in range(NY):
+                moved = value[part * blocks:(part + 1) * blocks]
+                shift = (part - kind) * ROWS % LANES
+                moved = pltpu.roll(moved, shift, 1) if shift else moved
+                row = jnp.where(segment == part, moved, row)
+            out[:, k, :] = row[:, :NY * ROWS]
 
 
 def per_device(queries, query_mass, first_range, library, library_mass, shuffle):
@@ -427,13 +427,13 @@
     hbm = pl.BlockSpec(memory_space=pl.ANY)
     dma = pltpu.SemaphoreType.DMA
     range_rows = NY * lib_rows
-    found = pl.pallas_call(
+    return tuple(pl.pallas_call(
         search_kernel,
-        out_shape=jax.ShapeDtypeStruct((NY, count, LANES), f32),
+        out_shape=(jax.ShapeDtypeStruct((count, TOP_HITS, q_rows), f32),) * 2,
         in_specs=[smem, hbm, vmem, hbm, hbm, vmem],
-        out_specs=vmem,
+        out_specs=(vmem, vmem),
         scratch_shapes=[
-            pltpu.VMEM((count, ROWS, depth), bf16),
+            pltpu.VMEM((count, NY, ROWS, depth), bf16),
             pltpu.VMEM((NZ * SLOTS, ROWS, depth), bf16),
             pltpu.VMEM((NZ, ROWS, LANES), bf16),
             pltpu.VMEM((NZ, SLOTS, ROWS, depth), bf16),
@@ -443,20 +443,18 @@
             pltpu.VMEM((NC, NY, 1, LANES), jnp.int32),
             pltpu.VMEM((NC, 2, range_rows, depth), bf16),
             pltpu.VMEM((depth, depth), bf16),
-            pltpu.VMEM((NC, LANES, depth), bf16),
+            pltpu.VMEM((2 * LANES, depth), bf16),
             pltpu.VMEM((NC, range_rows, LANES), f32),
             pltpu.VMEM((NC, range_rows, LANES), f32),
-            pltpu.VMEM((CHIPS, ROWS, LANES), f32),
-            pltpu.VMEM((NC, 2 * range_rows, LANES), f32),
+            pltpu.VMEM((NC, 2 * range_rows, 2 * LANES), f32),
             pltpu.VMEM((CHIPS, NC, 1, LANES), f32),
-            pltpu.VMEM((CHIPS * NC, 1, LANES), f32),
-            pltpu.VMEM((WINDOW, count, LANES), f32),
-            pltpu.VMEM((count * ROWS, LANES), f32),
-            pltpu.VMEM((count, LANES), f32),
-            pltpu.VMEM((NY, count, LANES), f32),
+            pltpu.VMEM((NY * CHIPS * NC, 1, LANES), f32),
+            pltpu.VMEM((WINDOW, NY * count, LANES), f32),
+            pltpu.VMEM((NY, count * ROWS, LANES), f32),
+            pltpu.VMEM((NY * count, LANES), f32),
             dma((NZ,)), dma((NZ,)), dma((NZ,)), dma((NZ,)),
             dma((NZ, NX)), dma((NZ, NX)), dma((NZ, NX)), dma((NZ, NX)), dma, dma,
-            dma((4,)), dma((4,)), dma((4,)), dma((4,)), dma((8,)), dma((8,)), dma((NY,)), dma((NY,)),
+            dma((4,)), dma((4,)), dma((4,)), dma((4,)), dma((8,)), dma((8,)),
             dma((3 + 2 * NZ,)),
         ],
         compiler_params=pltpu.CompilerParams(collective_id=0, has_side_effects=True),
@@ -464,10 +462,7 @@
     )(
         first_range, queries.reshape(count, NY, ROWS, depth), query_mass, library,
         library_mass.reshape(1, LANES), shuffle.reshape(1, depth),
-    )
-    found = found.reshape(NY, count, 16, ROWS)[:, :, :2 * TOP_HITS]
-    found = jnp.transpose(found, (1, 2, 0, 3)).reshape(count, 2 * TOP_HITS, q_rows)
-    return (found[:, :TOP_HITS], found[:, TOP_HITS:])
+    ))
 
 
 def solution(mesh):

time: 51.4 us -> 49.4 us (0.961)
  Pallas kernels: 48.2 us -> 46.5 us
    pallas_call x1, Pallas kernels: 48.2 us -> 46.5 us  [per_device(): pl.pallas_call(search_kernel, out_shape=(jax.ShapeDtypeStruct((count, TOP...]
    unnamed x2, local copies, waits for them, and re-layouts: 1.41 us -> 0.01 us
    pallas_call x1 -> x2, local copies, waits for them, and re-layouts: 0.88 us -> 2.12 us  [per_device(): pl.pallas_call(search_kernel, out_shape=(jax.ShapeDtypeStruct((count, TOP...]
where the time goes in v3:
time: 49.4 us; the launch traced here: 49.2 us
  Pallas kernels  46.5 us (94%)
  local copies, waits for them, and re-layouts  2.13 us (4%)
  between operations  0.65 us (1%)
    pallas_call x1, Pallas kernels, per_device(): pl.pallas_call(search_kernel, out_shape=(jax.ShapeDtypeStruct((count, TOP...  46.5 us
    pallas_call x2, local copies, waits for them, and re-layouts, per_device(): pl.pallas_call(search_kernel, out_shape=(jax.ShapeDtypeStruct((count, TOP...  2.12 us

profile of v3, /device:TPU:1, one launch (start us, length us, event | category | flops | bytes accessed | tf_op | source)
XLA Modules:
  0.0 49.2 jit_solution(7234129082783645056)
XLA Ops:
  0.6 46.5 %search.1 = (f32[16,5,32]{2,1,0:T(8,128)}, f32[16,5,32]{2,1,0:T(8,128)}) custom-call(s32[16]{0:T(128)} %first_ref.1, bf16[16,4,8,1024]{3,2,1,0:T(8,128)(2,1)} %bitcast.3, s32[16,32]{1,0:T(8,128)} %q_mass.1, bf16[128,1024]{1,0:T(8,128)(2,1)} %lib.1, s32[1,128]{1,0:T(1,128)} %bitcast.5, s32[1,1024]{1,0:T(1,128)} %bitcast.4), custom_call_target="tpu_custom_call" | custom-call | tf_op jit(solution)/shard_map/search/pallas_call | solution.py:430
  47.1 0.0 copy-start
  47.1 1.5 %copy.8 = f32[16,5,32]{2,0,1:T(8,128)} copy(f32[16,5,32]{2,1,0:T(8,128)} %get-tuple-element.2) | data formatting | bytes 20480 | tf_op jit(solution)/shard_map/search/pallas_call | solution.py:430
  48.6 0.0 copy-done
  48.6 0.6 %copy.9 = f32[16,5,32]{2,0,1:T(8,128)} copy(f32[16,5,32]{2,1,0:T(8,128)S(1)} %copy-done) | data formatting | bytes 20480 | tf_op jit(solution)/shard_map/search/pallas_call | solution.py:430
Async XLA Ops:
  47.1 1.5 %copy-start = (f32[16,5,32]{2,1,0:T(8,128)S(1)}, f32[16,5,32]{2,1,0:T(8,128)}, u32[]{:S(2)}) copy-start(f32[16,5,32]{2,1,0:T(8,128)} %get-tuple-element.3) | copy-start | bytes 30724

commit v4 on v3

--- a/solution.py
+++ b/solution.py
@@ -58,8 +58,8 @@
 
 
 def search_kernel(
-    first_ref, queries, q_mass, lib, lib_mass, shuffle, out_t, out_d,
-    qall, send, code, zbuf, zcode, qbuf, xcode, lmbuf, spectra, onehot, columns, scale_rep, mass_rep,
+    first_range, queries, query_mass, lib, lib_mass, shuffle, out,
+    first_ref, q_mass, names_ref, qall, send, code, zbuf, zcode, qbuf, xcode, lmbuf, spectra, onehot, columns, scale_rep, mass_rep,
     scores, obuf, rbuf, abuf, norms, q_scale,
     z_send, z_recv, zc_send, zc_recv, x_send, x_recv, xc_send, xc_recv, r_send, r_recv,
     l_send, l_recv, c_send, c_recv, lm_send, lm_recv, here_sem,
@@ -95,6 +95,11 @@
     for peer in peers:
         pl.semaphore_signal(barrier, inc=1, device_id=peer, device_id_type=MESH)
 
+    take_first = pltpu.make_async_copy(first_range, first_ref, here_sem.at[3])
+    take_q_mass = pltpu.make_async_copy(query_mass, q_mass, here_sem.at[4])
+    take_names = pltpu.make_async_copy(shuffle, names_ref, here_sem.at[5])
+    for copy in (take_first, take_q_mass, take_names):
+        copy.start()
     take_queries = pltpu.make_async_copy(queries, qall, here_sem.at[0])
     take_queries.start()
     own_lib = spectra.at[c, 0, pl.ds(y * lib_rows, lib_rows)]
@@ -102,6 +107,9 @@
     take_lib.start()
     take_mass = pltpu.make_async_copy(lib_mass, lmbuf.at[c, y], here_sem.at[2])
     take_mass.start()
+
+    take_first.wait()
+    take_q_mass.wait()
 
     lane = lax.broadcasted_iota(jnp.int32, (ROWS, LANES), 1)
     row8 = lax.broadcasted_iota(jnp.int32, (ROWS, LANES), 0)
@@ -142,6 +150,18 @@
         return carry
 
     lax.fori_loop(0, NZ * SLOTS, gather, 0)
+    chunk = 64
+    take_names.wait()
+    names = names_ref[...]
+
+    def build(i, carry):
+        base = pl.multiple_of(i * chunk, chunk)
+        index = lax.broadcasted_iota(jnp.int32, (chunk, depth), 0) + base
+        onehot[pl.ds(base, chunk), :] = jnp.where(index == names, 1.0, 0.0).astype(jnp.bfloat16)
+        return carry
+
+    lax.fori_loop(0, depth // chunk, build, 0)
+
     take_lib.wait()
     take_mass.wait()
 
@@ -182,10 +202,6 @@
         for dx in (2, 1, 3, 0):
             start(x_copies(at, dx))
 
-    for at in range(1, NZ):
-        start(z_copies(at))
-    forward(0)
-
     half = lib_rows // 2
     up, down, opposite = turn(y, 1, NY), turn(y, NY - 1, NY), turn(y, 2, NY)
 
@@ -200,6 +216,10 @@
     own_down = piece_copy(piece(y), l_sems, 1, (m, down))
     own_core = piece_copy(piece(y), c_sems, 0, (partner, y))
     start((own_up, own_down, own_core))
+    for at in range(1, NZ):
+        start(z_copies(at))
+    forward(0)
+
     lm_copies = []
     for core in range(NC):
         for step in range(NY):
@@ -211,17 +231,6 @@
                 ))
     start(lm_copies)
 
-    chunk = 64
-    names = shuffle[...]
-
-    def build(i, carry):
-        base = pl.multiple_of(i * chunk, chunk)
-        index = lax.broadcasted_iota(jnp.int32, (chunk, depth), 0) + base
-        onehot[pl.ds(base, chunk), :] = jnp.where(index == names, 1.0, 0.0).astype(jnp.bfloat16)
-        return carry
-
-    lax.fori_loop(0, depth // chunk, build, 0)
-
     def prepare(e, at):
         base = pl.multiple_of(at * lib_rows, lib_rows)
         rows = spectra[e, 0, pl.ds(base, lib_rows), :]
@@ -244,23 +253,6 @@
     prepare(c, y)
     arrive(3)
     arrive(4)
-
-    wide_row = lax.broadcasted_iota(jnp.int32, (blocks, LANES), 0)
-
-    def norm(i, carry):
-        part, b = i // (blocks // 2), (i % (blocks // 2)) * 2
-        wide = qall[pl.ds(b, 2), part].astype(jnp.float32).reshape(2 * ROWS, depth)
-        total = jnp.sum(wide * wide, axis=1, keepdims=True)
-        norms[part, pl.ds(pl.multiple_of(b * ROWS, 16), 16), :] = jnp.broadcast_to(
-            lax.rsqrt(total + epsilon), (2 * ROWS, LANES)
-        )
-        return carry
-
-    lax.fori_loop(0, NY * blocks // 2, norm, 0)
-    for part in range(NY):
-        q_scale[part * blocks:(part + 1) * blocks, :] = spread(
-            jnp.where(wide_lane // ROWS == wide_row, norms[part].T[:blocks], 0.0)
-        )
 
     own_up.wait_recv()
     relay_up = piece_copy(piece(down, 0, half), l_sems, 2, (m, up))
@@ -278,13 +270,13 @@
     prepare(c, up)
     core_down.wait_recv()
     prepare(1 - c, down)
-    arrive(7)
-    core_up.wait_recv()
-    prepare(1 - c, up)
     relay_up.wait_recv()
     relay_down.wait_recv()
     core_opposite = piece_copy(piece(opposite), c_sems, 3, (partner, y))
     core_opposite.start()
+    arrive(7)
+    core_up.wait_recv()
+    prepare(1 - c, up)
     prepare(c, opposite)
 
     for copy in lm_copies:
@@ -314,6 +306,18 @@
             tile = tile + xcode[at, dx].astype(jnp.float32)
         return tile
 
+    own_rows = (y * CHIPS + g) * NC
+
+    def give(at):
+        for dx in range(NX):
+            chip = turn(z, NZ - ORDER[at], NZ) * NX + turn(x, NX - dx, NX)
+            for step in (2, 1, 3, 0):
+                if at or dx or step:
+                    remote(
+                        obuf.at[at * NX + dx], rbuf.at[pl.ds(own_rows, NC)], r_send, r_recv,
+                        (chip * NC + c, turn(y, step, NY)),
+                    ).start()
+
     for lg in range(2):
         first_at = lg * NZ // 2
         combined = pack(first_at)
@@ -347,7 +351,7 @@
 
         nothing = jnp.full((ROWS, LANES), EMPTY, jnp.float32)
         best = lax.fori_loop(
-            0, range_rows // ROWS, scan, (nothing,) * (4 * TOP_HITS), unroll=2
+            0, range_rows // ROWS, scan, (nothing,) * (4 * TOP_HITS), unroll=8
         )
         for e in range(NC):
             lanes = []
@@ -364,17 +368,9 @@
             table = swap_blocks(jnp.concatenate([upper, lower], axis=0))
             for k in range(16):
                 obuf[lg * 16 + k, e] = table[k:k + 1, :]
-
-    own_rows = (y * CHIPS + g) * NC
-    for at in range(NZ - 1, -1, -1):
-        for dx in range(NX):
-            chip = turn(z, NZ - ORDER[at], NZ) * NX + turn(x, NX - dx, NX)
-            for step in (2, 1, 3, 0):
-                if at or dx or step:
-                    remote(
-                        obuf.at[at * NX + dx], rbuf.at[pl.ds(own_rows, NC)], r_send, r_recv,
-                        (chip * NC + c, turn(y, step, NY)),
-                    ).start()
+        for at in range(first_at + NZ // 2 - 1, first_at - 1, -1):
+            give(at)
+
     keep = pltpu.make_async_copy(obuf.at[0], rbuf.at[pl.ds(own_rows, NC)], here_sem.at[0])
     keep.start()
 
@@ -387,6 +383,23 @@
                 copy.wait_send()
     for copy in (own_up, own_down, relay_up, relay_down, own_core, core_down, core_up, core_opposite):
         copy.wait_send()
+
+    wide_row = lax.broadcasted_iota(jnp.int32, (blocks, LANES), 0)
+
+    def norm(i, carry):
+        part, b = i // (blocks // 2), (i % (blocks // 2)) * 2
+        wide = qall[pl.ds(b, 2), part].astype(jnp.float32).reshape(2 * ROWS, depth)
+        total = jnp.sum(wide * wide, axis=1, keepdims=True)
+        norms[part, pl.ds(pl.multiple_of(b * ROWS, 16), 16), :] = jnp.broadcast_to(
+            lax.rsqrt(total + epsilon), (2 * ROWS, LANES)
+        )
+        return carry
+
+    lax.fori_loop(0, NY * blocks // 2, norm, 0)
+    for part in range(NY):
+        q_scale[part * blocks:(part + 1) * blocks, :] = spread(
+            jnp.where(wide_lane // ROWS == wide_row, norms[part].T[:blocks], 0.0)
+        )
 
     keep.wait()
     for sem in (r_send, r_recv):
@@ -408,14 +421,14 @@
     segment = wide_lane // ROWS
     for k in range(TOP_HITS):
         value = jnp.where(best[k] <= 0.5 * EMPTY, floor_score, best[k] * scale)
-        for out, kind in ((out_t, 0), (out_d, TOP_HITS)):
+        for side in range(2):
             row = jnp.zeros((blocks, LANES), jnp.float32)
             for part in range(NY):
                 moved = value[part * blocks:(part + 1) * blocks]
-                shift = (part - kind) * ROWS % LANES
+                shift = (part - side * TOP_HITS) * ROWS % LANES
                 moved = pltpu.roll(moved, shift, 1) if shift else moved
                 row = jnp.where(segment == part, moved, row)
-            out[:, k, :] = row[:, :NY * ROWS]
+            out[side, k] = row[:, :NY * ROWS]
 
 
 def per_device(queries, query_mass, first_range, library, library_mass, shuffle):
@@ -423,16 +436,18 @@
     lib_rows = library.shape[0]
     f32, bf16 = jnp.float32, jnp.bfloat16
     vmem = pl.BlockSpec(memory_space=pltpu.VMEM)
-    smem = pl.BlockSpec(memory_space=pltpu.SMEM)
     hbm = pl.BlockSpec(memory_space=pl.ANY)
     dma = pltpu.SemaphoreType.DMA
     range_rows = NY * lib_rows
-    return tuple(pl.pallas_call(
+    found = pl.pallas_call(
         search_kernel,
-        out_shape=(jax.ShapeDtypeStruct((count, TOP_HITS, q_rows), f32),) * 2,
-        in_specs=[smem, hbm, vmem, hbm, hbm, vmem],
-        out_specs=(vmem, vmem),
+        out_shape=jax.ShapeDtypeStruct((2, TOP_HITS, count, q_rows), f32),
+        in_specs=[hbm] * 6,
+        out_specs=vmem,
         scratch_shapes=[
+            pltpu.SMEM((count,), jnp.int32),
+            pltpu.VMEM((count, q_rows), jnp.int32),
+            pltpu.VMEM((1, depth), jnp.int32),
             pltpu.VMEM((count, NY, ROWS, depth), bf16),
             pltpu.VMEM((NZ * SLOTS, ROWS, depth), bf16),
             pltpu.VMEM((NZ, ROWS, LANES), bf16),
@@ -462,7 +477,28 @@
     )(
         first_range, queries.reshape(count, NY, ROWS, depth), query_mass, library,
         library_mass.reshape(1, LANES), shuffle.reshape(1, depth),
-    ))
+    )
+    def settle(hits, out_t, out_d, held, sem_in, sem_out):
+        copy = pltpu.make_async_copy(hits, held, sem_in)
+        copy.start()
+        copy.wait()
+        copies = [
+            pltpu.make_async_copy(held.at[side], out, sem_out.at[side])
+            for side, out in enumerate((out_t, out_d))
+        ]
+        for copy in copies:
+            copy.start()
+        for copy in copies:
+            copy.wait()
+
+    parts = pl.pallas_call(
+        settle,
+        out_shape=(jax.ShapeDtypeStruct((TOP_HITS, count, q_rows), f32),) * 2,
+        in_specs=[hbm], out_specs=(hbm, hbm),
+        scratch_shapes=[pltpu.VMEM((2, TOP_HITS, count, q_rows), f32), dma, dma((2,))],
+        name="settle",
+    )(found)
+    return tuple(jnp.transpose(part, (1, 0, 2)) for part in parts)
 
 
 def solution(mesh):

time: 49.4 us -> 44.7 us (0.905)
  Pallas kernels: 46.5 us -> 43.9 us
  local copies, waits for them, and re-layouts: 2.13 us -> 0 us
    pallas_call x1 -> x2, Pallas kernels: 46.5 us -> 43.9 us  [the longest x1 42.4 us: per_device(): pl.pallas_call(search_kernel, out_shape=jax.ShapeDtypeStruct((2, TOP_HITS...]
    pallas_call x2 -> x0, local copies, waits for them, and re-layouts: 2.12 us -> none  [per_device(): pl.pallas_call(search_kernel, out_shape=(jax.ShapeDtypeStruct((count, TOP...]
where the time goes in v4:
time: 44.7 us; the launch traced here: 44.6 us
  Pallas kernels  43.9 us (98%)
  between operations  0.64 us (1%)
    pallas_call x1, Pallas kernels, per_device(): pl.pallas_call(search_kernel, out_shape=jax.ShapeDtypeStruct((2, TOP_HITS...  42.4 us
    pallas_call x1, Pallas kernels, per_device(): pl.pallas_call(settle, out_shape=(jax.ShapeDtypeStruct((TOP_HITS, count,...  1.54 us

profile of v4, /device:TPU:1, one launch (start us, length us, event | category | flops | bytes accessed | tf_op | source)
XLA Modules:
  0.0 44.6 jit_solution(9305440176843331766)
XLA Ops:
  0.6 42.4 %search.1.hits = f32[2,5,16,32]{3,2,1,0:T(8,128)} custom-call(s32[16]{0:T(128)} %first_range.1, bf16[16,4,8,1024]{3,2,1,0:T(8,128)(2,1)} %bitcast.5, s32[16,32]{1,0:T(8,128)} %query_mass.1, bf16[128,1024]{1,0:T(8,128)(2,1)} %lib.1, s32[1,128]{1,0:T(1,128)} %bitcast.7, s32[1,1024]{1,0:T(1,128)} %bitcast.6), custom_call_target="tpu_custom_call" | custom-call | tf_op jit(solution)/shard_map/search/pallas_call | solution.py:442
  43.0 1.5 %settle.1 = (f32[5,16,32]{2,1,0:T(8,128)}, f32[5,16,32]{2,1,0:T(8,128)}) custom-call(f32[2,5,16,32]{3,2,1,0:T(8,128)} %search.1.hits), custom_call_target="tpu_custom_call" | custom-call | tf_op jit(solution)/shard_map/settle/pallas_call | solution.py:494

commit v5 on v4

--- a/solution.py
+++ b/solution.py
@@ -266,14 +266,14 @@
     own_core.wait_recv()
     prepare(1 - c, y)
     prepare(c, down)
+    relay_up.wait_recv()
+    relay_down.wait_recv()
+    core_opposite = piece_copy(piece(opposite), c_sems, 3, (partner, y))
+    core_opposite.start()
     arrive(6)
     prepare(c, up)
     core_down.wait_recv()
     prepare(1 - c, down)
-    relay_up.wait_recv()
-    relay_down.wait_recv()
-    core_opposite = piece_copy(piece(opposite), c_sems, 3, (partner, y))
-    core_opposite.start()
     arrive(7)
     core_up.wait_recv()
     prepare(1 - c, up)
@@ -286,9 +286,6 @@
             mass = jnp.broadcast_to(lmbuf[e, at].astype(jnp.float32), (lib_rows, LANES)).T
             mass = mass + ((x * NC + e) * BINS).astype(jnp.float32) + OFFSET
             mass_rep[e, at * lib_rows:(at + 1) * lib_rows, :] = mass
-    core_opposite.wait_recv()
-    prepare(1 - c, opposite)
-
     def pack(at):
         for dx in range(NX):
             for copy in x_copies(at, dx):
@@ -306,6 +303,10 @@
             tile = tile + xcode[at, dx].astype(jnp.float32)
         return tile
 
+    early = pack(0) + pack(1) + pack(2) + pack(3)
+    core_opposite.wait_recv()
+    prepare(1 - c, opposite)
+
     own_rows = (y * CHIPS + g) * NC
 
     def give(at):
@@ -320,9 +321,7 @@
 
     for lg in range(2):
         first_at = lg * NZ // 2
-        combined = pack(first_at)
-        for at in range(first_at + 1, first_at + NZ // 2):
-            combined = combined + pack(at)
+        combined = pack(4) + pack(5) + pack(6) + pack(7) if lg else early
 
         masses = []
         others = []
@@ -368,9 +367,9 @@
             table = swap_blocks(jnp.concatenate([upper, lower], axis=0))
             for k in range(16):
                 obuf[lg * 16 + k, e] = table[k:k + 1, :]
-        for at in range(first_at + NZ // 2 - 1, first_at - 1, -1):
-            give(at)
-
+
+    for at in range(NZ - 1, -1, -1):
+        give(at)
     keep = pltpu.make_async_copy(obuf.at[0], rbuf.at[pl.ds(own_rows, NC)], here_sem.at[0])
     keep.start()
 

time: 44.7 us -> 43.9 us (0.982)
  Pallas kernels: 43.9 us -> 43 us
    pallas_call x1, Pallas kernels: 42.4 us -> 41.5 us  [per_device(): pl.pallas_call(search_kernel, out_shape=jax.ShapeDtypeStruct((2, TOP_HITS...]
where the time goes in v5:
time: 43.9 us; the launch traced here: 43.7 us
  Pallas kernels  43 us (98%)
  between operations  0.64 us (1%)
    pallas_call x1, Pallas kernels, per_device(): pl.pallas_call(search_kernel, out_shape=jax.ShapeDtypeStruct((2, TOP_HITS...  41.5 us
    pallas_call x1, Pallas kernels, per_device(): pl.pallas_call(settle, out_shape=(jax.ShapeDtypeStruct((TOP_HITS, count,...  1.54 us

profile of v5, /device:TPU:1, one launch (start us, length us, event | category | flops | bytes accessed | tf_op | source)
XLA Modules:
  0.0 43.7 jit_solution(1936170758663737100)
XLA Ops:
  0.6 41.5 %search.1.hits = f32[2,5,16,32]{3,2,1,0:T(8,128)} custom-call(s32[16]{0:T(128)} %first_range.1, bf16[16,4,8,1024]{3,2,1,0:T(8,128)(2,1)} %bitcast.5, s32[16,32]{1,0:T(8,128)} %query_mass.1, bf16[128,1024]{1,0:T(8,128)(2,1)} %lib.1, s32[1,128]{1,0:T(1,128)} %bitcast.7, s32[1,1024]{1,0:T(1,128)} %bitcast.6), custom_call_target="tpu_custom_call" | custom-call | tf_op jit(solution)/shard_map/search/pallas_call | solution.py:441
  42.1 1.5 %settle.1 = (f32[5,16,32]{2,1,0:T(8,128)}, f32[5,16,32]{2,1,0:T(8,128)}) custom-call(f32[2,5,16,32]{3,2,1,0:T(8,128)} %search.1.hits), custom_call_target="tpu_custom_call" | custom-call | tf_op jit(solution)/shard_map/settle/pallas_call | solution.py:493
